TPU v7x, 32 devices: a whole 2x2x4 slice. The times are simulated.
32 devices in a mesh: section: 4 (over y, x), dp: 8 (over z, core).
Axes of the slice: x: 2, y: 2, z: 4, core: 2. Of those that a mesh axis runs over, the one named last changes fastest.
Arguments:
- tokens: bfloat16 [3840, 2048], P('dp'), may hold values from -6 to 6
- cotangent: bfloat16 [3840, 2048], P('dp'), may hold values from -6 to 6
- w_gate: bfloat16 [4, 2048, 512], P('section'), may hold values from -0.125 to 0.125
- w_up: bfloat16 [4, 2048, 512], P('section'), may hold values from -0.125 to 0.125
- w_down: bfloat16 [4, 2048, 512], P('section'), may hold values from -0.25 to 0.25
Outputs:
- input_grad: bfloat16 [4, 3840, 2048], P('section', 'dp')
- grad_gate: float32 [4, 2048, 512], P('section', 'dp')
- grad_up: float32 [4, 2048, 512], P('section', 'dp')
- grad_down: float32 [4, 2048, 512], P('section', 'dp')
All inputs are finite; a program needn't handle non-finite values.
Results may differ from a plain program's by a relative error of at most 0.035.
Values may be sent and summed in bfloat16 or wider, within the bound.
No kernel may reach another device: no remote copies, remote signals or barrier semaphores. Data moves between devices by JAX's collectives and lax.ppermute only.
A program may use at most 128 MiB of HBM per device.

v0:
```python
import functools

import jax
import jax.numpy as jnp
from jax import lax
from jax.experimental import pallas as pl
from jax.experimental.pallas import tpu as pltpu
from jax.sharding import PartitionSpec as P


ROWS = 48
LAGS_F = (2, 2, 2)
LAGS_B = (2, 2, 2)
PIECES_F = 2
PIECES_B = 2


f32 = jnp.float32
bf16 = jnp.bfloat16
NT = (((1,), (1,)), ((), ()))
TN = (((0,), (0,)), ((), ()))
VM = pl.BlockSpec(memory_space=pltpu.VMEM)


def shape_of(*dims, dtype=bf16):
    return jax.ShapeDtypeStruct(dims, dtype)


def pieces(size, count, body):
    step = size // count
    if count == 1:
        body(pl.ds(0, size))
        return

    def one(i, carry):
        body(pl.ds(pl.multiple_of(i * step, step), step))
        return carry

    lax.fori_loop(0, count, one, 0)


def place_of(start, size):
    return pl.ds(start if isinstance(start, int) else pl.multiple_of(start, size), size)


def pick_of(place, values):
    result = values[0]
    for at, value in enumerate(values[1:]):
        result = jnp.where(place > at, value, result)
    return result


def lag_of(lags, hop):
    return lags[hop] if hop < len(lags) else lags[-1]


def starts_of(sections):
    last = sections - 1
    forward = [0]
    for hop in range(last):
        forward.append(forward[-1] + lag_of(LAGS_F, hop))
    backward = [forward[-1]]
    for hop in range(last):
        backward.append(backward[-1] + lag_of(LAGS_B, hop))
    return forward, backward[::-1]


def tick_kernel(tick, micro, rows, sections, plan, *refs):
    runs_f, runs_b, routes, arrivals, places, inputs, starts_f, starts_b = plan
    refs = list(refs)
    place = lax.axis_index("section")
    tokens = refs.pop(0) if inputs[0] else None
    cotangent = refs.pop(0) if inputs[1] else None
    w_gate, w_up, w_down = refs[:3]
    refs = refs[3:]
    arrived = [(refs.pop(0), takers) for takers in arrivals]
    saved = []
    for at in places:
        saved.append((at, refs[:3]))
        refs = refs[3:]
    outs = [refs.pop(0) for _ in routes]
    if runs_f:
        gate_f, up_f, x_f = refs[:3]
        refs = refs[3:]
    if runs_b:
        new_grad, norms, terms = refs[:3]
        refs = refs[3:]
    x_b, gate_b, up_b, grad_in, normed, hidden, wide = refs
    last = sections - 1
    units = w_gate.shape[1]
    index_f = tick - pick_of(place, starts_f)
    index_b = tick - pick_of(place, starts_b)

    def window(index, source):
        total = source.shape[0]
        start = jnp.clip(index * rows, 0, total - rows)
        return source[pl.ds(pl.multiple_of(start, 16), rows), :]

    good_f = (index_f >= 0) & (index_f < micro)
    good_b = (index_b >= 0) & (index_b < micro)

    def emit(kind, columns, value):
        for out, route in zip(outs, routes):
            senders = [s for s, what in route if what == kind]
            if senders:
                hit = functools.reduce(jnp.logical_or, [place == s for s in senders])

                @pl.when(hit)
                def send():
                    out[:, columns] = value

    def receive(kind, target, source, owner, index):
        if source is not None:

            @pl.when(place == owner)
            def own():
                target[...] = window(index, source)

        for value, takers in arrived:
            for s, what in takers:
                if what == kind:

                    @pl.when(place == s)
                    def passed():
                        target[...] = value[...]

    if runs_f:

        @pl.when(good_f)
        def forward():
            receive("x", x_f, tokens, 0, index_f)
            xf = x_f[...].astype(f32)
            scale = lax.rsqrt(jnp.mean(xf * xf, axis=-1, keepdims=True) + 1e-06)
            normed[...] = (xf * scale).astype(bf16)

            def entry(columns):
                value = normed[...]
                gate = jnp.dot(value, w_gate[:, columns], preferred_element_type=f32)
                upper = jnp.dot(value, w_up[:, columns], preferred_element_type=f32)
                gate_f[:, columns] = gate
                up_f[:, columns] = upper
                value = (gate * jax.nn.sigmoid(gate) * upper).astype(bf16)
                hidden[:, columns] = value

            pieces(units, PIECES_F, entry)

            @pl.when(place != last)
            def exit_():
                def down(columns):
                    branch = lax.dot_general(
                        hidden[...], w_down[columns, :], NT, preferred_element_type=f32
                    )
                    value = (x_f[:, columns].astype(f32) + branch).astype(bf16)
                    emit("x", columns, value)

                pieces(x_f.shape[1], PIECES_F, down)

    if runs_b:

        @pl.when(good_b)
        def backward():
            receive("b", grad_in, cotangent, last, index_b)
            for at, kept in saved:

                @pl.when(place == at)
                def take():
                    gate_b[...] = kept[0][...]
                    up_b[...] = kept[1][...]
                    x_b[...] = kept[2][...]

            if runs_f:

                @pl.when(place == last)
                def same():
                    gate_b[...] = gate_f[...]
                    up_b[...] = up_f[...]
                    x_b[...] = x_f[...]

            def entry(columns):
                d_hidden = jnp.dot(grad_in[...], w_down[:, columns], preferred_element_type=f32)
                gate = gate_b[:, columns]
                upper = up_b[:, columns]
                sig = jax.nn.sigmoid(gate)
                first = columns.start
                size = columns.size
                terms[:, columns] = (gate * sig * upper).astype(bf16)
                d_up = (d_hidden * gate * sig).astype(bf16)
                d_gate = (d_hidden * upper * sig * (1.0 + gate * (1.0 - sig))).astype(bf16)
                terms[:, place_of(units + first, size)] = d_up
                terms[:, place_of(2 * units + first, size)] = d_gate

            pieces(units, PIECES_B, entry)

            def exit_(columns):
                d_norm = lax.dot_general(
                    terms[:, pl.ds(2 * units, units)], w_gate[columns, :], NT, preferred_element_type=f32
                )
                d_norm = d_norm + lax.dot_general(
                    terms[:, pl.ds(units, units)], w_up[columns, :], NT, preferred_element_type=f32
                )
                wide[:, columns] = d_norm

            pieces(x_b.shape[1], PIECES_B, exit_)
            xf = x_b[...].astype(f32)
            scale = lax.rsqrt(jnp.mean(xf * xf, axis=-1, keepdims=True) + 1e-06)
            x_hat = xf * scale
            norms[...] = x_hat.astype(bf16)
            d_norm = wide[...]
            inner = jnp.mean(d_norm * x_hat, axis=-1, keepdims=True)
            grad = grad_in[...].astype(f32) + scale * (d_norm - x_hat * inner)
            grad = grad.astype(bf16)
            new_grad[...] = grad
            emit("b", pl.ds(0, x_b.shape[1]), grad)


def tick_call(tick, micro, rows, sections, arrays, routes, came, saved):
    _, width = arrays[0].shape
    units = arrays[2].shape[1]
    last = sections - 1
    starts_f, starts_b = starts_of(sections)
    runs_f = 0 <= tick < micro + starts_f[last]
    runs_b = 0 <= tick - starts_b[last] < micro + starts_b[0] - starts_b[last]
    own_f = 0 <= tick < micro
    own_b = 0 <= tick - starts_b[last] < micro
    places = [at for at, _ in saved]
    inputs = (own_f, own_b)
    operands = [a for a, used in zip(arrays, inputs) if used] + list(arrays[2:])
    operands += [value for value, _ in came]
    for _, kept in saved:
        operands += kept
    out_shape = [shape_of(rows, width)] * len(routes)
    if runs_f:
        out_shape += [shape_of(rows, units, dtype=f32)] * 2 + [shape_of(rows, width)]
    if runs_b:
        out_shape += [shape_of(rows, width), shape_of(rows, width), shape_of(rows, 3 * units)]
    plan = (
        runs_f,
        runs_b,
        routes,
        [takers for _, takers in came],
        places,
        inputs,
        starts_f,
        starts_b,
    )
    result = pl.pallas_call(
        functools.partial(tick_kernel, tick, micro, rows, sections, plan),
        out_shape=out_shape,
        in_specs=[VM] * len(operands),
        out_specs=[VM] * len(out_shape),
        scratch_shapes=[
            pltpu.VMEM((rows, width), bf16),
            pltpu.VMEM((rows, units), f32),
            pltpu.VMEM((rows, units), f32),
            pltpu.VMEM((rows, width), bf16),
            pltpu.VMEM((rows, width), bf16),
            pltpu.VMEM((rows, units), bf16),
            pltpu.VMEM((rows, width), f32),
        ],
        compiler_params=pltpu.CompilerParams(vmem_limit_bytes=10 << 20),
        cost_estimate=pl.CostEstimate(
            flops=6 * (runs_f + runs_b) * rows * width * units,
            bytes_accessed=6 * width * units,
            transcendentals=0,
        ),
        name="tick",
    )(*operands)
    result = list(result)
    outs = result[: len(routes)]
    rest = result[len(routes) :]
    kept = rest[:3] if runs_f else None
    terms = rest[-3:] if runs_b else None
    return outs, kept, terms


def collect_call(micro, rows, sections, total, whole, sources):
    last = sections - 1
    starts_b = starts_of(sections)[1]
    starts = [min(i * rows, total - rows) for i in range(micro)]
    whole = [] if whole is None else [whole]
    found = []
    at_of = {}
    for tick, value in enumerate(sources):
        by_place = value if isinstance(value, dict) else dict.fromkeys(range(sections), value)
        for at, array in by_place.items():
            known = [i for i, old in enumerate(found) if old is array]
            if not known:
                known = [len(found)]
                found.append(array)
            at_of[tick, at] = known[0]

    def kernel(*refs):
        place = lax.axis_index("section")
        target = refs[-1]
        pool = refs[len(whole) : -1]
        for at in range(sections):

            @pl.when(place == at)
            def take():
                if whole and at == last:
                    target[...] = refs[0][...]
                else:
                    for i, start in enumerate(starts):
                        target[start : start + rows, :] = pool[at_of[i + starts_b[at] - starts_b[last], at]][...]

    operands = whole + found
    width = operands[-1].shape[1]
    return pl.pallas_call(
        kernel,
        out_shape=shape_of(total, width),
        in_specs=[VM] * len(operands),
        out_specs=VM,
        compiler_params=pltpu.CompilerParams(vmem_limit_bytes=10 << 20),
        cost_estimate=pl.CostEstimate(flops=0, bytes_accessed=4 * total * width, transcendentals=0),
        name="collect",
    )(*operands)


def edges_of(sections):
    edges = [("x", at, at + 1) for at in range(sections - 1)]
    return edges + [("b", at, at - 1) for at in range(1, sections)]


def plan_routes(tick, micro, sections):
    starts_f, starts_b = starts_of(sections)
    edges = {}
    for kind, a, b in edges_of(sections):
        start = (starts_b if kind == "b" else starts_f)[a]
        if 0 <= tick - start < micro:
            edges[a, b] = kind
    plans = []
    both = [(a, b) for a, b in edges if a < b and (b, a) in edges]
    for parity in (0, 1):
        chosen = [p for a, b in both if a % 2 == parity for p in ((a, b), (b, a))]
        if chosen:
            plans.append({pair: edges.pop(pair) for pair in chosen})
    for kind in ("x", "b"):
        chosen = [pair for pair, what in edges.items() if what == kind]
        if chosen:
            plans.append({pair: kind for pair in chosen})
    routes = []
    for plan in plans:
        full = dict(plan)
        full = {a: b for a, b in full}
        targets = set(full.values())
        for a in sorted(full):
            if a not in targets:
                end = a
                while end in full:
                    end = full[end]
                full[end] = a
        routes.append((full, [(kind, a, b) for (a, b), kind in plan.items()]))
    return routes


def permute(value, full, sections, lanes):
    pairs = []
    for s in range(sections):
        for d in range(lanes):
            to = full[s] * lanes + d if s in full else s * lanes + (d ^ 1)
            pairs.append((s * lanes + d, to))
    return lax.ppermute(value, ("section", "dp"), pairs)


def weight_kernel(left, right, *refs):
    core = lax.rem(lax.axis_index("dp"), 2)
    keep, send = refs[-2:]
    half = keep.shape[1]
    both = lax.dot_general(left[...], right[...], TN, preferred_element_type=f32).astype(bf16)
    low, high = both[:half], both[half:]

    @pl.when(core == 0)
    def even():
        keep[0] = low
        send[0] = high

    @pl.when(core != 0)
    def odd():
        keep[0] = high
        send[0] = low


def weight_call(chips, left, right, right_at, units, after):
    total, width = left.shape
    pair = width // chips
    half = pair // 2
    return pl.pallas_call(
        weight_kernel,
        out_shape=[shape_of(chips, half, units)] * 2,
        grid=(chips,),
        in_specs=[
            pl.BlockSpec((total, pair), lambda i: (0, i)),
            pl.BlockSpec((total, units), lambda i: (0, right_at)),
        ]
        + [pl.BlockSpec(memory_space=pl.ANY)] * len(after),
        out_specs=[pl.BlockSpec((1, half, units), lambda i: (i, 0, 0))] * 2,
        compiler_params=pltpu.CompilerParams(vmem_limit_bytes=10 << 20),
        cost_estimate=pl.CostEstimate(
            flops=2 * total * width * units, bytes_accessed=4 * width * units, transcendentals=0
        ),
        name="weight",
    )(left, right, *after)


def from_sides(chip, chips, arrived):
    first = arrived[0][...].astype(f32)
    second = arrived[1][...].astype(f32) if len(arrived) > 1 else first
    even = lax.rem(chip, 2) == 0
    left = jnp.where(chip > 0, jnp.where(even, second, first), 0.0)
    right = jnp.where(chip < chips - 1, jnp.where(even, first, second), 0.0)
    return left, right


def step_kernel(step, chips, keep, swapped, *refs):
    chip = lax.div(lax.axis_index("dp"), 2)
    even = lax.rem(chip, 2) == 0
    outs = refs[-2:]
    arrived = refs[:-2]
    to_right = jnp.clip(chips - step + chip, 0, chips - 1)
    to_left = jnp.clip(step - chips + chip, 0, chips - 1)
    right = keep[to_right].astype(f32) + swapped[to_right].astype(f32)
    left = keep[to_left].astype(f32) + swapped[to_left].astype(f32)
    if arrived:
        from_left, from_right = from_sides(chip, chips, arrived)
        right = right + jnp.where(chip <= step - 1, from_left, 0.0)
        left = left + jnp.where(chip >= chips - step, from_right, 0.0)
    outs[0][...] = jnp.where(even, right, left).astype(bf16)
    outs[1][...] = jnp.where(even, left, right).astype(bf16)


def step_call(step, chips, keep, swapped, arrived):
    half, units = keep.shape[1:]
    return pl.pallas_call(
        functools.partial(step_kernel, step, chips),
        out_shape=[shape_of(half, units)] * 2,
        in_specs=[VM] * (2 + len(arrived)),
        out_specs=[VM, VM],
        compiler_params=pltpu.CompilerParams(vmem_limit_bytes=10 << 20),
        cost_estimate=pl.CostEstimate(flops=half * units, bytes_accessed=half * units, transcendentals=0),
        name="step",
    )(keep, swapped, *arrived)


def final_kernel(chips, keep, swapped, *refs):
    chip = lax.div(lax.axis_index("dp"), 2)
    from_left, from_right = from_sides(chip, chips, refs[:-1])
    refs[-1][...] = keep[chip].astype(f32) + swapped[chip].astype(f32) + from_left + from_right


def final_call(chips, keep, swapped, arrived):
    half, units = keep.shape[1:]
    return pl.pallas_call(
        functools.partial(final_kernel, chips),
        out_shape=shape_of(half, units, dtype=f32),
        in_specs=[VM] * (2 + len(arrived)),
        out_specs=VM,
        compiler_params=pltpu.CompilerParams(vmem_limit_bytes=10 << 20),
        cost_estimate=pl.CostEstimate(flops=half * units, bytes_accessed=half * units, transcendentals=0),
        name="final",
    )(keep, swapped, *arrived)


def body(tokens, cotangent, w_gate, w_up, w_down):
    sections = lax.axis_size("section")
    lanes = lax.axis_size("dp")
    chips = lanes // 2
    total, _ = tokens.shape
    units = w_gate.shape[2]
    rows = ROWS
    micro = -(-total // rows)
    last = sections - 1
    arrays = (tokens, cotangent, w_gate[0], w_up[0], w_down[0])

    starts_f, starts_b = starts_of(sections)
    sent, kept = {}, {}
    arrivals, history = [], []
    for tick in range(micro + starts_b[0]):
        routes = plan_routes(tick, micro, sections)
        came, into = [], {}
        for kind, a, b in edges_of(sections):
            starts = starts_b if kind == "b" else starts_f
            if 0 <= tick - starts[b] < micro:
                value = sent[kind, a, b, tick - starts[b] + starts[a]]
                takers = [old for array, old in came if array is value]
                if not takers:
                    takers = [[]]
                    came.append((value, takers[0]))
                takers[0].append((b, kind))
                if kind == "b":
                    into[b] = value
        saved = []
        for at in range(last):
            index = tick - starts_b[at]
            if 0 <= index < micro:
                saved.append((at, kept[index + starts_f[at]]))
        outs, kept[tick], terms = tick_call(
            tick,
            micro,
            rows,
            sections,
            arrays,
            [[(a, kind) for kind, a, _ in taken] for _, taken in routes],
            came,
            saved,
        )
        if terms is not None:
            history.append(terms)
            arrivals.append(into)
        for out, (full, taken) in zip(outs, routes):
            value = permute(out, full, sections, lanes)
            for kind, a, b in taken:
                sent[kind, a, b, tick] = value

    laid = functools.partial(collect_call, micro, rows, sections, total)
    all_in = collect_call(micro, rows, sections, total, arrays[1], arrivals)
    all_grad, normed, terms = [laid(None, list(column)) for column in zip(*history)]
    near = [(z, z ^ 1) for z in range(chips)]
    far = [(z, ((z + 1) ^ 1) - 1) for z in range(chips)]
    held = []

    def begin(which, after):
        left = all_in if which == 0 else normed
        keep, send = weight_call(chips, left, terms, which, units, after)
        held.append((keep, permute(send, {}, sections, lanes)))

    def advance(step, which, arrived):
        keep, swapped = held[which]
        outs = step_call(step, chips, keep, swapped, arrived)
        arrived = [line(outs[0], near, chips)]
        if step > 1 or chips % 2:
            arrived.append(line(outs[1], far, chips))
        return outs[0], arrived

    begin(0, [])
    begin(1, [])
    moving = []
    out, arrived = advance(1, 0, [])
    moving.append(arrived)
    begin(2, [out])
    moving.append(advance(1, 1, [])[1])
    moving.append(advance(1, 2, [])[1])
    for step in range(2, chips):
        for which in range(3):
            moving[which] = advance(step, which, moving[which])[1]
    results = [final_call(chips, *held[which], moving[which]) for which in range(3)]
    grad_d, grad_u, grad_g = results
    return (all_grad[None], grad_g[None], grad_u[None], grad_d[None])


def line(value, pairs, chips):
    route = []
    for z, to in pairs:
        for c in range(2):
            route.append((2 * z + c, 2 * to + c if 0 <= to < chips else 2 * z + 1 - c))
    return lax.ppermute(value, "dp", route)


def solution(mesh):
    placed = (
        P("dp", None),
        P("dp", None),
        P("section", None, None),
        P("section", None, None),
        P("section", None, None),
    )
    return jax.shard_map(
        body,
        mesh=mesh,
        in_specs=placed,
        out_specs=(
            P("section", "dp", None),
            P("section", "dp", None),
            P("section", "dp", None),
            P("section", "dp", None),
        ),
        check_vma=False,
    )
```

profile of v0, /device:TPU:0, one launch (start us, length us, event | category | flops | bytes accessed | tf_op | source)
XLA Modules:
  0.0 198.2 jit_solution(16017511344957773366)
XLA Ops:
  12.0 4.8 %collective-permute-done.3.refs_4_ = bf16[48,2048]{1,0:T(8,128)(2,1)S(1)} collective-permute-done((bf16[48,2048]{1,0:T(8,128)(2,1)S(1)}, bf16[48,2048]{1,0:T(8,128)(2,1)S(1)}, u32[]{:S(2)}, u32[]{:S(2)}) %collective-permute-start.3) | collective-permute-done | bytes 196640 | tf_op jit(solution)/shard_map/ppermute | solution.py:362
  27.8 3.3 %collective-permute-done.1.refs_4_ = bf16[48,2048]{1,0:T(8,128)(2,1)S(1)} collective-permute-done((bf16[48,2048]{1,0:T(8,128)(2,1)S(1)}, bf16[48,2048]{1,0:T(8,128)(2,1)S(1)}, u32[]{:S(2)}, u32[]{:S(2)}) %collective-permute-start.1) | collective-permute-done | bytes 196640 | tf_op jit(solution)/shard_map/ppermute | solution.py:362
  36.4 5.1 %collective-permute-done.2.refs_5_ = bf16[48,2048]{1,0:T(8,128)(2,1)S(1)} collective-permute-done((bf16[48,2048]{1,0:T(8,128)(2,1)S(1)}, bf16[48,2048]{1,0:T(8,128)(2,1)S(1)}, u32[]{:S(2)}, u32[]{:S(2)}) %collective-permute-start.2) | collective-permute-done | bytes 196640 | tf_op jit(solution)/shard_map/ppermute | solution.py:362
  56.5 7.3 %collective-permute-done.10.refs_4_ = bf16[48,2048]{1,0:T(8,128)(2,1)S(1)} collective-permute-done((bf16[48,2048]{1,0:T(8,128)(2,1)S(1)}, bf16[48,2048]{1,0:T(8,128)(2,1)S(1)}, u32[]{:S(2)}, u32[]{:S(2)}) %collective-permute-start.10) | collective-permute-done | bytes 196640 | tf_op jit(solution)/shard_map/ppermute | solution.py:362
  63.8 3.4 %collective-permute-start.21 = (bf16[48,2048]{1,0:T(8,128)(2,1)S(1)}, bf16[48,2048]{1,0:T(8,128)(2,1)S(1)}, u32[]{:S(2)}, u32[]{:S(2)}) collective-permute-start(bf16[48,2048]{1,0:T(8,128)(2,1)S(1)} %get-tuple-element.199), channel_id=1, source_target_pairs={{0,8},{1,9},{2,10},{3,11},{4,12},{5,13},{6,14},{7,15},{8,0},{9,1},... | collective-permute-start | bytes 589832 | tf_op jit(solution)/shard_map/ppermute | solution.py:362
  67.8 7.7 %collective-permute-start.18 = (bf16[48,2048]{1,0:T(8,128)(2,1)S(1)}, bf16[48,2048]{1,0:T(8,128)(2,1)S(1)}, u32[]{:S(2)}, u32[]{:S(2)}) collective-permute-start(bf16[48,2048]{1,0:T(8,128)(2,1)S(1)} %get-tuple-element.189), channel_id=1, source_target_pairs={{0,8},{1,9},{2,10},{3,11},{4,12},{5,13},{6,14},{7,15},{8,0},{9,1},... | collective-permute-start | bytes 589832 | tf_op jit(solution)/shard_map/ppermute | solution.py:362
  78.4 5.5 %collective-permute-start.25 = (bf16[48,2048]{1,0:T(8,128)(2,1)S(1)}, bf16[48,2048]{1,0:T(8,128)(2,1)S(1)}, u32[]{:S(2)}, u32[]{:S(2)}) collective-permute-start(bf16[48,2048]{1,0:T(8,128)(2,1)S(1)} %get-tuple-element.214), channel_id=1, source_target_pairs={{0,16},{1,17},{2,18},{3,19},{4,20},{5,21},{6,22},{7,23},{8,0},{9,1... | collective-permute-start | bytes 589832 | tf_op jit(solution)/shard_map/ppermute | solution.py:362
  87.7 4.6 %collective-permute-start.23 = (bf16[48,2048]{1,0:T(8,128)(2,1)S(1)}, bf16[48,2048]{1,0:T(8,128)(2,1)S(1)}, u32[]{:S(2)}, u32[]{:S(2)}) collective-permute-start(bf16[48,2048]{1,0:T(8,128)(2,1)S(1)} %get-tuple-element.208), channel_id=1, source_target_pairs={{0,16},{1,17},{2,18},{3,19},{4,20},{5,21},{6,22},{7,23},{8,0},{9,1... | collective-permute-start | bytes 589832 | tf_op jit(solution)/shard_map/ppermute | solution.py:362
  92.3 3.1 %tick.37 = (bf16[48,2048]{1,0:T(8,128)(2,1)S(1)}, f32[48,512]{1,0:T(8,128)}, f32[48,512]{1,0:T(8,128)}, bf16[48,2048]{1,0:T(8,128)(2,1)}, bf16[48,2048]{1,0:T(8,...) custom-call(bf16[480,2048]{1,0:T(8,128)(2,1)S(1)} %copy-done.6, ...), custom_call_target="tpu_custom_call" | custom-call | flops 603979776 | bytes 6291456 | tf_op jit(solution)/shard_map/tick/pallas_call | solution.py:246
  96.6 3.1 %tick.36 = (bf16[48,2048]{1,0:T(8,128)(2,1)S(1)}, f32[48,512]{1,0:T(8,128)}, f32[48,512]{1,0:T(8,128)}, bf16[48,2048]{1,0:T(8,128)(2,1)}, bf16[48,2048]{1,0:T(8,...) custom-call(bf16[480,2048]{1,0:T(8,128)(2,1)S(1)} %copy-done.6, ...), custom_call_target="tpu_custom_call" | custom-call | flops 603979776 | bytes 6291456 | tf_op jit(solution)/shard_map/tick/pallas_call | solution.py:246
  99.8 5.3 %collective-permute-start.26 = (bf16[48,2048]{1,0:T(8,128)(2,1)S(1)}, bf16[48,2048]{1,0:T(8,128)(2,1)S(1)}, u32[]{:S(2)}, u32[]{:S(2)}) collective-permute-start(bf16[48,2048]{1,0:T(8,128)(2,1)S(1)} %get-tuple-element.219), channel_id=1, source_target_pairs={{0,24},{1,25},{2,26},{3,27},{4,28},{5,29},{6,30},{7,31},{8,0},{9,1... | collective-permute-start | bytes 589832 | tf_op jit(solution)/shard_map/ppermute | solution.py:362
  107.4 4.6 %collective-permute-start.29 = (bf16[48,2048]{1,0:T(8,128)(2,1)S(1)}, bf16[48,2048]{1,0:T(8,128)(2,1)S(1)}, u32[]{:S(2)}, u32[]{:S(2)}) collective-permute-start(bf16[48,2048]{1,0:T(8,128)(2,1)S(1)} %get-tuple-element.231), channel_id=1, source_target_pairs={{0,16},{1,17},{2,18},{3,19},{4,20},{5,21},{6,22},{7,23},{8,0},{9,1... | collective-permute-start | bytes 589832 | tf_op jit(solution)/shard_map/ppermute | solution.py:362
  119.4 2.7 %collective-permute-start.31 = (bf16[48,2048]{1,0:T(8,128)(2,1)S(1)}, bf16[48,2048]{1,0:T(8,128)(2,1)S(1)}, u32[]{:S(2)}, u32[]{:S(2)}) collective-permute-start(bf16[48,2048]{1,0:T(8,128)(2,1)S(1)} %get-tuple-element.235), channel_id=1, source_target_pairs={{0,8},{1,9},{2,10},{3,11},{4,12},{5,13},{6,14},{7,15},{8,0},{9,1},... | collective-permute-start | bytes 589832 | tf_op jit(solution)/shard_map/ppermute | solution.py:362
  124.6 3.0 %collective-permute-start.30 = (bf16[48,2048]{1,0:T(8,128)(2,1)S(1)}, bf16[48,2048]{1,0:T(8,128)(2,1)S(1)}, u32[]{:S(2)}, u32[]{:S(2)}) collective-permute-start(bf16[48,2048]{1,0:T(8,128)(2,1)S(1)} %get-tuple-element.233), channel_id=1, source_target_pairs={{0,8},{1,9},{2,10},{3,11},{4,12},{5,13},{6,14},{7,15},{8,0},{9,1},... | collective-permute-start | bytes 589832 | tf_op jit(solution)/shard_map/ppermute | solution.py:362
  127.6 2.6 %tick.43 = (bf16[48,2048]{1,0:T(8,128)(2,1)S(1)}, bf16[48,2048]{1,0:T(8,128)(2,1)S(1)}, bf16[48,1536]{1,0:T(8,128)(2,1)S(1)}) custom-call(bf16[2048,512]{1,0:T(8,128)(2,1)S(1)} %bitcast.27, bf16[2048,512]{1,0:T(8,128)(2,1)S(1)} %bitcast.49, bf16[2048,512]{1,0:T(8,128)(2,1)S(1)} %bitcast.71, bf16[48,2048]{1,0:T(8,128)(2,1)S(1)} %collective-permute-done.31.refs_3_.refs_22_, ...), custom_call_target="tpu_custom_call" | custom-call | flops 301989888 | bytes 6291456 | tf_op jit(solution)/shard_map/tick/pallas_call | solution.py:246
  149.0 3.5 %collective-permute-done.45.refs_0_ = bf16[256,512]{1,0:T(8,128)(2,1)S(1)} collective-permute-done((bf16[256,512]{1,0:T(8,128)(2,1)S(1)}, bf16[256,512]{1,0:T(8,128)(2,1)S(1)}, u32[]{:S(2)}, u32[]{:S(2)}) %collective-permute-start.45) | collective-permute-done | bytes 262176 | tf_op jit(solution)/shard_map/ppermute | solution.py:555
  154.9 3.2 %collective-permute-done.40.refs_0_ = bf16[256,512]{1,0:T(8,128)(2,1)S(1)} collective-permute-done((bf16[256,512]{1,0:T(8,128)(2,1)S(1)}, bf16[256,512]{1,0:T(8,128)(2,1)S(1)}, u32[]{:S(2)}, u32[]{:S(2)}) %collective-permute-start.40) | collective-permute-done | bytes 262176 | tf_op jit(solution)/shard_map/ppermute | solution.py:555
  160.5 3.2 %collective-permute-done.34.refs_0_ = bf16[256,512]{1,0:T(8,128)(2,1)S(1)} collective-permute-done((bf16[256,512]{1,0:T(8,128)(2,1)S(1)}, bf16[256,512]{1,0:T(8,128)(2,1)S(1)}, u32[]{:S(2)}, u32[]{:S(2)}) %collective-permute-start.34) | collective-permute-done | bytes 262176 | tf_op jit(solution)/shard_map/ppermute | solution.py:555
  166.1 3.2 %collective-permute-done.46.refs_0_ = bf16[256,512]{1,0:T(8,128)(2,1)S(1)} collective-permute-done((bf16[256,512]{1,0:T(8,128)(2,1)S(1)}, bf16[256,512]{1,0:T(8,128)(2,1)S(1)}, u32[]{:S(2)}, u32[]{:S(2)}) %collective-permute-start.46) | collective-permute-done | bytes 262176 | tf_op jit(solution)/shard_map/ppermute | solution.py:555
  169.7 3.7 %collective-permute-start.48 = (bf16[256,512]{1,0:T(8,128)(2,1)S(1)}, bf16[256,512]{1,0:T(8,128)(2,1)S(1)}, u32[]{:S(2)}, u32[]{:S(2)}) collective-permute-start(bf16[256,512]{1,0:T(8,128)(2,1)S(1)} %get-tuple-element.288), channel_id=1, source_target_pairs={{0,2},{1,3},{2,0},{3,1},{4,6},{5,7},{6,4},{7,5},{8,10},{9,11},{10,... | collective-permute-start | bytes 786440 | tf_op jit(solution)/shard_map/ppermute | solution.py:555
  175.3 3.7 %collective-permute-start.43 = (bf16[256,512]{1,0:T(8,128)(2,1)S(1)}, bf16[256,512]{1,0:T(8,128)(2,1)S(1)}, u32[]{:S(2)}, u32[]{:S(2)}) collective-permute-start(bf16[256,512]{1,0:T(8,128)(2,1)S(1)} %get-tuple-element.284), channel_id=1, source_target_pairs={{0,2},{1,3},{2,0},{3,1},{4,6},{5,7},{6,4},{7,5},{8,10},{9,11},{10,... | collective-permute-start | bytes 786440 | tf_op jit(solution)/shard_map/ppermute | solution.py:555
  180.9 3.7 %collective-permute-start.37 = (bf16[256,512]{1,0:T(8,128)(2,1)S(1)}, bf16[256,512]{1,0:T(8,128)(2,1)S(1)}, u32[]{:S(2)}, u32[]{:S(2)}) collective-permute-start(bf16[256,512]{1,0:T(8,128)(2,1)S(1)} %get-tuple-element.277), channel_id=1, source_target_pairs={{0,2},{1,3},{2,0},{3,1},{4,6},{5,7},{6,4},{7,5},{8,10},{9,11},{10,... | collective-permute-start | bytes 786440 | tf_op jit(solution)/shard_map/ppermute | solution.py:555
  188.6 3.2 %collective-permute-done.43.refs_0_ = bf16[256,512]{1,0:T(8,128)(2,1)S(1)} collective-permute-done((bf16[256,512]{1,0:T(8,128)(2,1)S(1)}, bf16[256,512]{1,0:T(8,128)(2,1)S(1)}, u32[]{:S(2)}, u32[]{:S(2)}) %collective-permute-start.43) | collective-permute-done | bytes 262176 | tf_op jit(solution)/shard_map/ppermute | solution.py:555
  192.8 4.3 %collective-permute-done.37.refs_0_ = bf16[256,512]{1,0:T(8,128)(2,1)S(1)} collective-permute-done((bf16[256,512]{1,0:T(8,128)(2,1)S(1)}, bf16[256,512]{1,0:T(8,128)(2,1)S(1)}, u32[]{:S(2)}, u32[]{:S(2)}) %collective-permute-start.37) | collective-permute-done | bytes 262176 | tf_op jit(solution)/shard_map/ppermute | solution.py:555
  (133 shorter events, 99.4 us)
Async XLA Ops:
  55.2 12.1 %collective-permute-start.11 = (bf16[48,2048]{1,0:T(8,128)(2,1)S(1)}, bf16[48,2048]{1,0:T(8,128)(2,1)S(1)}, u32[]{:S(2)}, u32[]{:S(2)}) collective-permute-start(bf16[48,2048]{1,0:T(8,128)(2,1)S(1)} %get-tuple-element.168), channel_id=1, source_target_pairs={{0,1},{1,0},{2,3},{3,2},{4,5},{5,4},{6,7},{7,6},{8,16},{9,17},{10,... | collective-permute-start | bytes 589832 | tf_op jit(solution)/shard_map/ppermute | solution.py:362
  55.4 11.9 %collective-permute-start.12 = (bf16[48,2048]{1,0:T(8,128)(2,1)S(1)}, bf16[48,2048]{1,0:T(8,128)(2,1)S(1)}, u32[]{:S(2)}, u32[]{:S(2)}) collective-permute-start(bf16[48,2048]{1,0:T(8,128)(2,1)S(1)} %get-tuple-element.169), channel_id=1, source_target_pairs={{0,1},{1,0},{2,3},{3,2},{4,5},{5,4},{6,7},{7,6},{8,9},{9,8},{10,11... | collective-permute-start | bytes 589832 | tf_op jit(solution)/shard_map/ppermute | solution.py:362
  55.9 11.8 %collective-permute-start.19 = (bf16[48,2048]{1,0:T(8,128)(2,1)S(1)}, bf16[48,2048]{1,0:T(8,128)(2,1)S(1)}, u32[]{:S(2)}, u32[]{:S(2)}) collective-permute-start(bf16[48,2048]{1,0:T(8,128)(2,1)S(1)} %get-tuple-element.197), channel_id=1, source_target_pairs={{0,1},{1,0},{2,3},{3,2},{4,5},{5,4},{6,7},{7,6},{8,16},{9,17},{10,... | collective-permute-start | bytes 589832 | tf_op jit(solution)/shard_map/ppermute | solution.py:362
  56.2 19.3 %collective-permute-start.20 = (bf16[48,2048]{1,0:T(8,128)(2,1)S(1)}, bf16[48,2048]{1,0:T(8,128)(2,1)S(1)}, u32[]{:S(2)}, u32[]{:S(2)}) collective-permute-start(bf16[48,2048]{1,0:T(8,128)(2,1)S(1)} %get-tuple-element.198), channel_id=1, source_target_pairs={{0,1},{1,0},{2,3},{3,2},{4,5},{5,4},{6,7},{7,6},{8,9},{9,8},{10,11... | collective-permute-start | bytes 589832 | tf_op jit(solution)/shard_map/ppermute | solution.py:362
  63.8 12.1 %collective-permute-start.21 = (bf16[48,2048]{1,0:T(8,128)(2,1)S(1)}, bf16[48,2048]{1,0:T(8,128)(2,1)S(1)}, u32[]{:S(2)}, u32[]{:S(2)}) collective-permute-start(bf16[48,2048]{1,0:T(8,128)(2,1)S(1)} %get-tuple-element.199), channel_id=1, source_target_pairs={{0,8},{1,9},{2,10},{3,11},{4,12},{5,13},{6,14},{7,15},{8,0},{9,1},... | collective-permute-start | bytes 589832 | tf_op jit(solution)/shard_map/ppermute | solution.py:362
  67.3 16.6 %collective-permute-start.16 = (bf16[48,2048]{1,0:T(8,128)(2,1)S(1)}, bf16[48,2048]{1,0:T(8,128)(2,1)S(1)}, u32[]{:S(2)}, u32[]{:S(2)}) collective-permute-start(bf16[48,2048]{1,0:T(8,128)(2,1)S(1)} %get-tuple-element.187), channel_id=1, source_target_pairs={{0,1},{1,0},{2,3},{3,2},{4,5},{5,4},{6,7},{7,6},{8,16},{9,17},{10,... | collective-permute-start | bytes 589832 | tf_op jit(solution)/shard_map/ppermute | solution.py:362
  67.5 16.4 %collective-permute-start.17 = (bf16[48,2048]{1,0:T(8,128)(2,1)S(1)}, bf16[48,2048]{1,0:T(8,128)(2,1)S(1)}, u32[]{:S(2)}, u32[]{:S(2)}) collective-permute-start(bf16[48,2048]{1,0:T(8,128)(2,1)S(1)} %get-tuple-element.188), channel_id=1, source_target_pairs={{0,1},{1,0},{2,3},{3,2},{4,5},{5,4},{6,7},{7,6},{8,9},{9,8},{10,11... | collective-permute-start | bytes 589832 | tf_op jit(solution)/shard_map/ppermute | solution.py:362
  67.8 17.5 %collective-permute-start.18 = (bf16[48,2048]{1,0:T(8,128)(2,1)S(1)}, bf16[48,2048]{1,0:T(8,128)(2,1)S(1)}, u32[]{:S(2)}, u32[]{:S(2)}) collective-permute-start(bf16[48,2048]{1,0:T(8,128)(2,1)S(1)} %get-tuple-element.189), channel_id=1, source_target_pairs={{0,8},{1,9},{2,10},{3,11},{4,12},{5,13},{6,14},{7,15},{8,0},{9,1},... | collective-permute-start | bytes 589832 | tf_op jit(solution)/shard_map/ppermute | solution.py:362
  78.3 14.0 %collective-permute-start.24 = (bf16[48,2048]{1,0:T(8,128)(2,1)S(1)}, bf16[48,2048]{1,0:T(8,128)(2,1)S(1)}, u32[]{:S(2)}, u32[]{:S(2)}) collective-permute-start(bf16[48,2048]{1,0:T(8,128)(2,1)S(1)} %get-tuple-element.213), channel_id=1, source_target_pairs={{0,1},{1,0},{2,3},{3,2},{4,5},{5,4},{6,7},{7,6},{8,9},{9,8},{10,11... | collective-permute-start | bytes 589832 | tf_op jit(solution)/shard_map/ppermute | solution.py:362
  78.4 13.9 %collective-permute-start.25 = (bf16[48,2048]{1,0:T(8,128)(2,1)S(1)}, bf16[48,2048]{1,0:T(8,128)(2,1)S(1)}, u32[]{:S(2)}, u32[]{:S(2)}) collective-permute-start(bf16[48,2048]{1,0:T(8,128)(2,1)S(1)} %get-tuple-element.214), channel_id=1, source_target_pairs={{0,16},{1,17},{2,18},{3,19},{4,20},{5,21},{6,22},{7,23},{8,0},{9,1... | collective-permute-start | bytes 589832 | tf_op jit(solution)/shard_map/ppermute | solution.py:362
  99.8 13.7 %collective-permute-start.26 = (bf16[48,2048]{1,0:T(8,128)(2,1)S(1)}, bf16[48,2048]{1,0:T(8,128)(2,1)S(1)}, u32[]{:S(2)}, u32[]{:S(2)}) collective-permute-start(bf16[48,2048]{1,0:T(8,128)(2,1)S(1)} %get-tuple-element.219), channel_id=1, source_target_pairs={{0,24},{1,25},{2,26},{3,27},{4,28},{5,29},{6,30},{7,31},{8,0},{9,1... | collective-permute-start | bytes 589832 | tf_op jit(solution)/shard_map/ppermute | solution.py:362
  146.2 11.9 %collective-permute-start.40 = (bf16[256,512]{1,0:T(8,128)(2,1)S(1)}, bf16[256,512]{1,0:T(8,128)(2,1)S(1)}, u32[]{:S(2)}, u32[]{:S(2)}) collective-permute-start(bf16[256,512]{1,0:T(8,128)(2,1)S(1)} %get-tuple-element.281), channel_id=1, source_target_pairs={{0,2},{1,3},{2,0},{3,1},{4,6},{5,7},{6,4},{7,5},{8,10},{9,11},{10,... | collective-permute-start | bytes 786440 | tf_op jit(solution)/shard_map/ppermute | solution.py:555
  147.0 16.7 %collective-permute-start.34 = (bf16[256,512]{1,0:T(8,128)(2,1)S(1)}, bf16[256,512]{1,0:T(8,128)(2,1)S(1)}, u32[]{:S(2)}, u32[]{:S(2)}) collective-permute-start(bf16[256,512]{1,0:T(8,128)(2,1)S(1)} %get-tuple-element.274), channel_id=1, source_target_pairs={{0,2},{1,3},{2,0},{3,1},{4,6},{5,7},{6,4},{7,5},{8,10},{9,11},{10,... | collective-permute-start | bytes 786440 | tf_op jit(solution)/shard_map/ppermute | solution.py:555
  152.8 16.6 %collective-permute-start.46 = (bf16[256,512]{1,0:T(8,128)(2,1)S(1)}, bf16[256,512]{1,0:T(8,128)(2,1)S(1)}, u32[]{:S(2)}, u32[]{:S(2)}) collective-permute-start(bf16[256,512]{1,0:T(8,128)(2,1)S(1)} %get-tuple-element.286), channel_id=1, source_target_pairs={{0,2},{1,3},{2,0},{3,1},{4,6},{5,7},{6,4},{7,5},{8,10},{9,11},{10,... | collective-permute-start | bytes 786440 | tf_op jit(solution)/shard_map/ppermute | solution.py:555
  154.9 14.5 %collective-permute-start.47 = (bf16[256,512]{1,0:T(8,128)(2,1)S(1)}, bf16[256,512]{1,0:T(8,128)(2,1)S(1)}, u32[]{:S(2)}, u32[]{:S(2)}) collective-permute-start(bf16[256,512]{1,0:T(8,128)(2,1)S(1)} %get-tuple-element.287), channel_id=1, source_target_pairs={{0,1},{1,0},{2,4},{3,5},{4,2},{5,3},{6,7},{7,6},{8,9},{9,8},{10,12... | collective-permute-start | bytes 786440 | tf_op jit(solution)/shard_map/ppermute | solution.py:555
  158.4 16.6 %collective-permute-start.41 = (bf16[256,512]{1,0:T(8,128)(2,1)S(1)}, bf16[256,512]{1,0:T(8,128)(2,1)S(1)}, u32[]{:S(2)}, u32[]{:S(2)}) collective-permute-start(bf16[256,512]{1,0:T(8,128)(2,1)S(1)} %get-tuple-element.282), channel_id=1, source_target_pairs={{0,2},{1,3},{2,0},{3,1},{4,6},{5,7},{6,4},{7,5},{8,10},{9,11},{10,... | collective-permute-start | bytes 786440 | tf_op jit(solution)/shard_map/ppermute | solution.py:555
  160.5 14.5 %collective-permute-start.42 = (bf16[256,512]{1,0:T(8,128)(2,1)S(1)}, bf16[256,512]{1,0:T(8,128)(2,1)S(1)}, u32[]{:S(2)}, u32[]{:S(2)}) collective-permute-start(bf16[256,512]{1,0:T(8,128)(2,1)S(1)} %get-tuple-element.283), channel_id=1, source_target_pairs={{0,1},{1,0},{2,4},{3,5},{4,2},{5,3},{6,7},{7,6},{8,9},{9,8},{10,12... | collective-permute-start | bytes 786440 | tf_op jit(solution)/shard_map/ppermute | solution.py:555
  164.0 16.6 %collective-permute-start.35 = (bf16[256,512]{1,0:T(8,128)(2,1)S(1)}, bf16[256,512]{1,0:T(8,128)(2,1)S(1)}, u32[]{:S(2)}, u32[]{:S(2)}) collective-permute-start(bf16[256,512]{1,0:T(8,128)(2,1)S(1)} %get-tuple-element.275), channel_id=1, source_target_pairs={{0,2},{1,3},{2,0},{3,1},{4,6},{5,7},{6,4},{7,5},{8,10},{9,11},{10,... | collective-permute-start | bytes 786440 | tf_op jit(solution)/shard_map/ppermute | solution.py:555
  169.3 11.2 %collective-permute-start.36 = (bf16[256,512]{1,0:T(8,128)(2,1)S(1)}, bf16[256,512]{1,0:T(8,128)(2,1)S(1)}, u32[]{:S(2)}, u32[]{:S(2)}) collective-permute-start(bf16[256,512]{1,0:T(8,128)(2,1)S(1)} %get-tuple-element.276), channel_id=1, source_target_pairs={{0,1},{1,0},{2,4},{3,5},{4,2},{5,3},{6,7},{7,6},{8,9},{9,8},{10,12... | collective-permute-start | bytes 786440 | tf_op jit(solution)/shard_map/ppermute | solution.py:555
  169.7 16.5 %collective-permute-start.48 = (bf16[256,512]{1,0:T(8,128)(2,1)S(1)}, bf16[256,512]{1,0:T(8,128)(2,1)S(1)}, u32[]{:S(2)}, u32[]{:S(2)}) collective-permute-start(bf16[256,512]{1,0:T(8,128)(2,1)S(1)} %get-tuple-element.288), channel_id=1, source_target_pairs={{0,2},{1,3},{2,0},{3,1},{4,6},{5,7},{6,4},{7,5},{8,10},{9,11},{10,... | collective-permute-start | bytes 786440 | tf_op jit(solution)/shard_map/ppermute | solution.py:555
  175.0 12.7 %collective-permute-start.49 = (bf16[256,512]{1,0:T(8,128)(2,1)S(1)}, bf16[256,512]{1,0:T(8,128)(2,1)S(1)}, u32[]{:S(2)}, u32[]{:S(2)}) collective-permute-start(bf16[256,512]{1,0:T(8,128)(2,1)S(1)} %get-tuple-element.289), channel_id=1, source_target_pairs={{0,1},{1,0},{2,4},{3,5},{4,2},{5,3},{6,7},{7,6},{8,9},{9,8},{10,12... | collective-permute-start | bytes 786440 | tf_op jit(solution)/shard_map/ppermute | solution.py:555
  175.3 16.5 %collective-permute-start.43 = (bf16[256,512]{1,0:T(8,128)(2,1)S(1)}, bf16[256,512]{1,0:T(8,128)(2,1)S(1)}, u32[]{:S(2)}, u32[]{:S(2)}) collective-permute-start(bf16[256,512]{1,0:T(8,128)(2,1)S(1)} %get-tuple-element.284), channel_id=1, source_target_pairs={{0,2},{1,3},{2,0},{3,1},{4,6},{5,7},{6,4},{7,5},{8,10},{9,11},{10,... | collective-permute-start | bytes 786440 | tf_op jit(solution)/shard_map/ppermute | solution.py:555
  180.6 11.2 %collective-permute-start.44 = (bf16[256,512]{1,0:T(8,128)(2,1)S(1)}, bf16[256,512]{1,0:T(8,128)(2,1)S(1)}, u32[]{:S(2)}, u32[]{:S(2)}) collective-permute-start(bf16[256,512]{1,0:T(8,128)(2,1)S(1)} %get-tuple-element.285), channel_id=1, source_target_pairs={{0,1},{1,0},{2,4},{3,5},{4,2},{5,3},{6,7},{7,6},{8,9},{9,8},{10,12... | collective-permute-start | bytes 786440 | tf_op jit(solution)/shard_map/ppermute | solution.py:555
  180.9 16.2 %collective-permute-start.37 = (bf16[256,512]{1,0:T(8,128)(2,1)S(1)}, bf16[256,512]{1,0:T(8,128)(2,1)S(1)}, u32[]{:S(2)}, u32[]{:S(2)}) collective-permute-start(bf16[256,512]{1,0:T(8,128)(2,1)S(1)} %get-tuple-element.277), channel_id=1, source_target_pairs={{0,2},{1,3},{2,0},{3,1},{4,6},{5,7},{6,4},{7,5},{8,10},{9,11},{10,... | collective-permute-start | bytes 786440 | tf_op jit(solution)/shard_map/ppermute | solution.py:555
  (34 other events, 229.9 us)
where the time goes:
time: 198 us
  starting transfers between devices  71.5 us (36%)
  Pallas kernels  62.2 us (31%)
  waiting for transfers between devices  57.2 us (29%)
  local copies, waits for them, and re-layouts  6.33 us (3%)
    ppermute x35, starting transfers between devices, permute(): return lax.ppermute(value, ('section', 'dp'), pairs)  49.6 us
    pallas_call x22, Pallas kernels, tick_call(): pl.pallas_call(functools.partial(tick_kernel, tick, micro, rows, sections...  45.8 us
    ppermute x35, waiting for transfers between devices, permute(): return lax.ppermute(value, ('section', 'dp'), pairs)  31.8 us
    ppermute x15, waiting for transfers between devices, line(): return lax.ppermute(value, 'dp', route)  25.4 us
    ppermute x15, starting transfers between devices, line(): return lax.ppermute(value, 'dp', route)  21.9 us
    pallas_call x3, Pallas kernels, weight_call(): pl.pallas_call(weight_kernel, out_shape=[shape_of(chips, half, units)] *...  7.06 us
    unnamed x16, local copies, waits for them, and re-layouts  6.33 us
    pallas_call x9, Pallas kernels, step_call(): pl.pallas_call(functools.partial(step_kernel, step, chips), out_shape=[sh...  4.46 us
  transfers between devices with their start and end apart: 50, of which 25 were waited for; matrix products, arithmetic and copies ran while one was open for 0% of the time, Pallas kernels for 27%

commit v1 on v0

--- a/solution.py
+++ b/solution.py
@@ -11,6 +11,7 @@
 ROWS = 48
 LAGS_F = (2, 2, 2)
 LAGS_B = (2, 2, 2)
+LOAD_MIB = 44
 PIECES_F = 2
 PIECES_B = 2
 
@@ -20,6 +21,7 @@
 NT = (((1,), (1,)), ((), ()))
 TN = (((0,), (0,)), ((), ()))
 VM = pl.BlockSpec(memory_space=pltpu.VMEM)
+ANY = pl.BlockSpec(memory_space=pl.ANY)
 
 
 def shape_of(*dims, dtype=bf16):
@@ -66,13 +68,17 @@
 
 
 def tick_kernel(tick, micro, rows, sections, plan, *refs):
-    runs_f, runs_b, routes, arrivals, places, inputs, starts_f, starts_b = plan
+    runs_f, runs_b, routes, arrivals, places, inputs, starts_f, starts_b, loading = plan
     refs = list(refs)
     place = lax.axis_index("section")
     tokens = refs.pop(0) if inputs[0] else None
     cotangent = refs.pop(0) if inputs[1] else None
     w_gate, w_up, w_down = refs[:3]
     refs = refs[3:]
+    loads = []
+    if loading:
+        sems = refs.pop()
+        sources = [tokens.at[pl.ds(0, rows), :], w_gate, w_up, w_down]
     arrived = [(refs.pop(0), takers) for takers in arrivals]
     saved = []
     for at in places:
@@ -85,6 +91,14 @@
     if runs_b:
         new_grad, norms, terms = refs[:3]
         refs = refs[3:]
+    if loading:
+        w_gate, w_up, w_down = refs[:3]
+        refs = refs[3:]
+        targets = [x_f, w_gate, w_up, w_down]
+        for number in range(4):
+            copy = pltpu.make_async_copy(sources[number], targets[number], sems.at[number])
+            copy.start()
+            loads.append(copy)
     x_b, gate_b, up_b, grad_in, normed, hidden, wide = refs
     last = sections - 1
     units = w_gate.shape[1]
@@ -128,7 +142,10 @@
 
         @pl.when(good_f)
         def forward():
-            receive("x", x_f, tokens, 0, index_f)
+            if loading:
+                loads[0].wait()
+            else:
+                receive("x", x_f, tokens, 0, index_f)
             xf = x_f[...].astype(f32)
             scale = lax.rsqrt(jnp.mean(xf * xf, axis=-1, keepdims=True) + 1e-06)
             normed[...] = (xf * scale).astype(bf16)
@@ -142,7 +159,11 @@
                 value = (gate * jax.nn.sigmoid(gate) * upper).astype(bf16)
                 hidden[:, columns] = value
 
+            for copy in loads[1:3]:
+                copy.wait()
             pieces(units, PIECES_F, entry)
+            for copy in loads[3:]:
+                copy.wait()
 
             @pl.when(place != last)
             def exit_():
@@ -154,6 +175,13 @@
                     emit("x", columns, value)
 
                 pieces(x_f.shape[1], PIECES_F, down)
+
+    if loading:
+
+        @pl.when(jnp.logical_not(good_f))
+        def idle():
+            for copy in loads:
+                copy.wait()
 
     if runs_b:
 
@@ -233,6 +261,9 @@
         out_shape += [shape_of(rows, units, dtype=f32)] * 2 + [shape_of(rows, width)]
     if runs_b:
         out_shape += [shape_of(rows, width), shape_of(rows, width), shape_of(rows, 3 * units)]
+    loading = tick == 0
+    if loading:
+        out_shape += [shape_of(*w.shape) for w in arrays[2:]]
     plan = (
         runs_f,
         runs_b,
@@ -242,11 +273,12 @@
         inputs,
         starts_f,
         starts_b,
+        loading,
     )
     result = pl.pallas_call(
         functools.partial(tick_kernel, tick, micro, rows, sections, plan),
         out_shape=out_shape,
-        in_specs=[VM] * len(operands),
+        in_specs=[ANY if loading else VM] * len(operands),
         out_specs=[VM] * len(out_shape),
         scratch_shapes=[
             pltpu.VMEM((rows, width), bf16),
@@ -256,8 +288,9 @@
             pltpu.VMEM((rows, width), bf16),
             pltpu.VMEM((rows, units), bf16),
             pltpu.VMEM((rows, width), f32),
-        ],
-        compiler_params=pltpu.CompilerParams(vmem_limit_bytes=10 << 20),
+        ]
+        + [pltpu.SemaphoreType.DMA((4,))] * loading,
+        compiler_params=pltpu.CompilerParams(vmem_limit_bytes=(LOAD_MIB if loading else 10) << 20),
         cost_estimate=pl.CostEstimate(
             flops=6 * (runs_f + runs_b) * rows * width * units,
             bytes_accessed=6 * width * units,
@@ -268,9 +301,12 @@
     result = list(result)
     outs = result[: len(routes)]
     rest = result[len(routes) :]
+    loaded = None
+    if loading:
+        rest, loaded = rest[:-3], rest[-3:]
     kept = rest[:3] if runs_f else None
     terms = rest[-3:] if runs_b else None
-    return outs, kept, terms
+    return outs, kept, terms, loaded
 
 
 def collect_call(micro, rows, sections, total, whole, sources):
@@ -380,23 +416,30 @@
         send[0] = low
 
 
-def weight_call(chips, left, right, right_at, units, after):
+def weight_call(chips, left, right, right_at, units, after, ends=False):
     total, width = left.shape
     pair = width // chips
     half = pair // 2
+    count = 2 if ends else chips
+
+    def column(i):
+        return (0, (chips - 1) * (1 - i) if ends else i)
+
     return pl.pallas_call(
         weight_kernel,
-        out_shape=[shape_of(chips, half, units)] * 2,
-        grid=(chips,),
+        out_shape=[shape_of(count, half, units)] * 2,
+        grid=(count,),
         in_specs=[
-            pl.BlockSpec((total, pair), lambda i: (0, i)),
+            pl.BlockSpec((total, pair), column),
             pl.BlockSpec((total, units), lambda i: (0, right_at)),
         ]
         + [pl.BlockSpec(memory_space=pl.ANY)] * len(after),
         out_specs=[pl.BlockSpec((1, half, units), lambda i: (i, 0, 0))] * 2,
         compiler_params=pltpu.CompilerParams(vmem_limit_bytes=10 << 20),
         cost_estimate=pl.CostEstimate(
-            flops=2 * total * width * units, bytes_accessed=4 * width * units, transcendentals=0
+            flops=2 * total * pair * count * units,
+            bytes_accessed=4 * pair * count * units,
+            transcendentals=0,
         ),
         name="weight",
     )(left, right, *after)
@@ -416,8 +459,11 @@
     even = lax.rem(chip, 2) == 0
     outs = refs[-2:]
     arrived = refs[:-2]
-    to_right = jnp.clip(chips - step + chip, 0, chips - 1)
-    to_left = jnp.clip(step - chips + chip, 0, chips - 1)
+    if keep.shape[0] < chips:
+        to_right, to_left = 0, 1
+    else:
+        to_right = jnp.clip(chips - step + chip, 0, chips - 1)
+        to_left = jnp.clip(step - chips + chip, 0, chips - 1)
     right = keep[to_right].astype(f32) + swapped[to_right].astype(f32)
     left = keep[to_left].astype(f32) + swapped[to_left].astype(f32)
     if arrived:
@@ -493,7 +539,7 @@
             index = tick - starts_b[at]
             if 0 <= index < micro:
                 saved.append((at, kept[index + starts_f[at]]))
-        outs, kept[tick], terms = tick_call(
+        outs, kept[tick], terms, loaded = tick_call(
             tick,
             micro,
             rows,
@@ -503,6 +549,8 @@
             came,
             saved,
         )
+        if loaded is not None:
+            arrays = (tokens, cotangent, *loaded)
         if terms is not None:
             history.append(terms)
             arrivals.append(into)
@@ -516,29 +564,30 @@
     all_grad, normed, terms = [laid(None, list(column)) for column in zip(*history)]
     near = [(z, z ^ 1) for z in range(chips)]
     far = [(z, ((z + 1) ^ 1) - 1) for z in range(chips)]
-    held = []
+    held = {}
 
     def begin(which, after):
         left = all_in if which == 0 else normed
         keep, send = weight_call(chips, left, terms, which, units, after)
-        held.append((keep, permute(send, {}, sections, lanes)))
-
-    def advance(step, which, arrived):
-        keep, swapped = held[which]
+        held[which] = (keep, permute(send, {}, sections, lanes))
+
+    def advance(step, which, arrived, quick=None):
+        keep, swapped = quick or held[which]
         outs = step_call(step, chips, keep, swapped, arrived)
         arrived = [line(outs[0], near, chips)]
         if step > 1 or chips % 2:
             arrived.append(line(outs[1], far, chips))
         return outs[0], arrived
 
-    begin(0, [])
-    begin(1, [])
-    moving = []
-    out, arrived = advance(1, 0, [])
-    moving.append(arrived)
+    keep, send = weight_call(chips, all_in, terms, 0, units, [], True)
+    quick = (keep, permute(send, {}, sections, lanes))
+    begin(1, [send])
+    moving = {}
+    out, moving[0] = advance(1, 0, [], quick)
     begin(2, [out])
-    moving.append(advance(1, 1, [])[1])
-    moving.append(advance(1, 2, [])[1])
+    out, moving[1] = advance(1, 1, [])
+    begin(0, [out])
+    moving[2] = advance(1, 2, [])[1]
     for step in range(2, chips):
         for which in range(3):
             moving[which] = advance(step, which, moving[which])[1]

time: 198 us -> 201 us (1.015)
  starting transfers between devices: 71.5 us -> 85.7 us
  waiting for transfers between devices: 57.2 us -> 46.8 us
  local copies, waits for them, and re-layouts: 6.33 us -> 1.54 us
  Pallas kernels: 62.2 us -> 65.5 us
    ppermute x35 -> x36, starting transfers between devices: 49.6 us -> 61.7 us  [permute(): return lax.ppermute(value, ('section', 'dp'), pairs)]
    ppermute x35 -> x36, waiting for transfers between devices: 31.8 us -> 22.4 us  [permute(): return lax.ppermute(value, ('section', 'dp'), pairs)]
    unnamed x16 -> x4, local copies, waits for them, and re-layouts: 6.33 us -> 1.54 us
    ppermute x15, starting transfers between devices: 21.9 us -> 24 us  [line(): return lax.ppermute(value, 'dp', route)]
    pallas_call x22, Pallas kernels: 45.8 us -> 47.9 us  [tick_call(): pl.pallas_call(functools.partial(tick_kernel, tick, micro, rows, sections...]
    pallas_call x3 -> x4, Pallas kernels: 7.06 us -> 8.25 us  [weight_call(): pl.pallas_call(weight_kernel, out_shape=[shape_of(count, half, units)] *...]
  transfers between devices with their start and end apart: 50 -> 51, of which waited for: 25 -> 23; matrix products, arithmetic and copies ran while one was open for 0% -> 0% of each run, Pallas kernels for 27% -> 27%
where the time goes in v1:
time: 201 us; the launch traced here: 200 us
  starting transfers between devices  85.7 us (43%)
  Pallas kernels  65.5 us (33%)
  waiting for transfers between devices  46.8 us (23%)
    ppermute x36, starting transfers between devices, permute(): return lax.ppermute(value, ('section', 'dp'), pairs)  61.7 us
    pallas_call x22, Pallas kernels, tick_call(): pl.pallas_call(functools.partial(tick_kernel, tick, micro, rows, sections...  47.9 us
    ppermute x15, waiting for transfers between devices, line(): return lax.ppermute(value, 'dp', route)  24.4 us
    ppermute x15, starting transfers between devices, line(): return lax.ppermute(value, 'dp', route)  24 us
    ppermute x36, waiting for transfers between devices, permute(): return lax.ppermute(value, ('section', 'dp'), pairs)  22.4 us
    pallas_call x4, Pallas kernels, weight_call(): pl.pallas_call(weight_kernel, out_shape=[shape_of(count, half, units)] *...  8.25 us
    pallas_call x9, Pallas kernels, step_call(): pl.pallas_call(functools.partial(step_kernel, step, chips), out_shape=[sh...  4.47 us
  transfers between devices with their start and end apart: 51, of which 23 were waited for; matrix products, arithmetic and copies ran while one was open for 0% of the time, Pallas kernels for 27%

profile of v1, /device:TPU:0, one launch (start us, length us, event | category | flops | bytes accessed | tf_op | source)
XLA Modules:
  0.0 200.5 jit_solution(8069301938260057025)
XLA Ops:
  2.2 4.3 %tick.22 = (bf16[48,2048]{1,0:T(8,128)(2,1)S(1)}, f32[48,512]{1,0:T(8,128)S(1)}, f32[48,512]{1,0:T(8,128)S(1)}, bf16[48,2048]{1,0:T(8,128)(2,1)S(1)}, bf16[2048,...) custom-call(bf16[480,2048]{1,0:T(8,128)(2,1)S(1)} %copy-done.1, ...), custom_call_target="tpu_custom_call" | custom-call | flops 301989888 | bytes 6291456 | tf_op jit(solution)/shard_map/tick/pallas_call | solution.py:278
  10.4 3.9 %collective-permute-done.refs_4_ = bf16[48,2048]{1,0:T(8,128)(2,1)S(1)} collective-permute-done((bf16[48,2048]{1,0:T(8,128)(2,1)S(1)}, bf16[48,2048]{1,0:T(8,128)(2,1)S(1)}, u32[]{:S(2)}, u32[]{:S(2)}) %collective-permute-start) | collective-permute-done | bytes 196640 | tf_op jit(solution)/shard_map/ppermute | solution.py:398
  47.4 4.4 %collective-permute-start.13 = (bf16[48,2048]{1,0:T(8,128)(2,1)S(1)}, bf16[48,2048]{1,0:T(8,128)(2,1)S(1)}, u32[]{:S(2)}, u32[]{:S(2)}) collective-permute-start(bf16[48,2048]{1,0:T(8,128)(2,1)S(1)} %get-tuple-element.185), channel_id=1, source_target_pairs={{0,8},{1,9},{2,10},{3,11},{4,12},{5,13},{6,14},{7,15},{8,0},{9,1},... | collective-permute-start | bytes 589832 | tf_op jit(solution)/shard_map/ppermute | solution.py:398
  52.8 6.6 %collective-permute-done.13.refs_4_ = bf16[48,2048]{1,0:T(8,128)(2,1)S(1)} collective-permute-done((bf16[48,2048]{1,0:T(8,128)(2,1)S(1)}, bf16[48,2048]{1,0:T(8,128)(2,1)S(1)}, u32[]{:S(2)}, u32[]{:S(2)}) %collective-permute-start.13) | collective-permute-done | bytes 196640 | tf_op jit(solution)/shard_map/ppermute | solution.py:398
  59.4 4.2 %collective-permute-start.18 = (bf16[48,2048]{1,0:T(8,128)(2,1)S(1)}, bf16[48,2048]{1,0:T(8,128)(2,1)S(1)}, u32[]{:S(2)}, u32[]{:S(2)}) collective-permute-start(bf16[48,2048]{1,0:T(8,128)(2,1)S(1)} %get-tuple-element.197), channel_id=1, source_target_pairs={{0,8},{1,9},{2,10},{3,11},{4,12},{5,13},{6,14},{7,15},{8,0},{9,1},... | collective-permute-start | bytes 589832 | tf_op jit(solution)/shard_map/ppermute | solution.py:398
  64.2 7.9 %collective-permute-start.21 = (bf16[48,2048]{1,0:T(8,128)(2,1)S(1)}, bf16[48,2048]{1,0:T(8,128)(2,1)S(1)}, u32[]{:S(2)}, u32[]{:S(2)}) collective-permute-start(bf16[48,2048]{1,0:T(8,128)(2,1)S(1)} %get-tuple-element.207), channel_id=1, source_target_pairs={{0,8},{1,9},{2,10},{3,11},{4,12},{5,13},{6,14},{7,15},{8,0},{9,1},... | collective-permute-start | bytes 589832 | tf_op jit(solution)/shard_map/ppermute | solution.py:398
  74.9 5.6 %collective-permute-start.23 = (bf16[48,2048]{1,0:T(8,128)(2,1)S(1)}, bf16[48,2048]{1,0:T(8,128)(2,1)S(1)}, u32[]{:S(2)}, u32[]{:S(2)}) collective-permute-start(bf16[48,2048]{1,0:T(8,128)(2,1)S(1)} %get-tuple-element.216), channel_id=1, source_target_pairs={{0,16},{1,17},{2,18},{3,19},{4,20},{5,21},{6,22},{7,23},{8,0},{9,1... | collective-permute-start | bytes 589832 | tf_op jit(solution)/shard_map/ppermute | solution.py:398
  84.3 4.6 %collective-permute-start.25 = (bf16[48,2048]{1,0:T(8,128)(2,1)S(1)}, bf16[48,2048]{1,0:T(8,128)(2,1)S(1)}, u32[]{:S(2)}, u32[]{:S(2)}) collective-permute-start(bf16[48,2048]{1,0:T(8,128)(2,1)S(1)} %get-tuple-element.222), channel_id=1, source_target_pairs={{0,16},{1,17},{2,18},{3,19},{4,20},{5,21},{6,22},{7,23},{8,0},{9,1... | collective-permute-start | bytes 589832 | tf_op jit(solution)/shard_map/ppermute | solution.py:398
  88.9 3.1 %tick.36 = (bf16[48,2048]{1,0:T(8,128)(2,1)S(1)}, f32[48,512]{1,0:T(8,128)}, f32[48,512]{1,0:T(8,128)}, bf16[48,2048]{1,0:T(8,128)(2,1)}, bf16[48,2048]{1,0:T(8,...) custom-call(bf16[480,2048]{1,0:T(8,128)(2,1)S(1)} %copy-done, ...), custom_call_target="tpu_custom_call" | custom-call | flops 603979776 | bytes 6291456 | tf_op jit(solution)/shard_map/tick/pallas_call | solution.py:278
  93.2 3.1 %tick.37 = (bf16[48,2048]{1,0:T(8,128)(2,1)S(1)}, f32[48,512]{1,0:T(8,128)}, f32[48,512]{1,0:T(8,128)}, bf16[48,2048]{1,0:T(8,128)(2,1)}, bf16[48,2048]{1,0:T(8,...) custom-call(bf16[480,2048]{1,0:T(8,128)(2,1)S(1)} %copy-done, ...), custom_call_target="tpu_custom_call" | custom-call | flops 603979776 | bytes 6291456 | tf_op jit(solution)/shard_map/tick/pallas_call | solution.py:278
  96.4 5.3 %collective-permute-start.27 = (bf16[48,2048]{1,0:T(8,128)(2,1)S(1)}, bf16[48,2048]{1,0:T(8,128)(2,1)S(1)}, u32[]{:S(2)}, u32[]{:S(2)}) collective-permute-start(bf16[48,2048]{1,0:T(8,128)(2,1)S(1)} %get-tuple-element.232), channel_id=1, source_target_pairs={{0,24},{1,25},{2,26},{3,27},{4,28},{5,29},{6,30},{7,31},{8,0},{9,1... | collective-permute-start | bytes 589832 | tf_op jit(solution)/shard_map/ppermute | solution.py:398
  104.0 4.6 %collective-permute-start.28 = (bf16[48,2048]{1,0:T(8,128)(2,1)S(1)}, bf16[48,2048]{1,0:T(8,128)(2,1)S(1)}, u32[]{:S(2)}, u32[]{:S(2)}) collective-permute-start(bf16[48,2048]{1,0:T(8,128)(2,1)S(1)} %get-tuple-element.237), channel_id=1, source_target_pairs={{0,16},{1,17},{2,18},{3,19},{4,20},{5,21},{6,22},{7,23},{8,0},{9,1... | collective-permute-start | bytes 589832 | tf_op jit(solution)/shard_map/ppermute | solution.py:398
  121.2 3.0 %collective-permute-start.31 = (bf16[48,2048]{1,0:T(8,128)(2,1)S(1)}, bf16[48,2048]{1,0:T(8,128)(2,1)S(1)}, u32[]{:S(2)}, u32[]{:S(2)}) collective-permute-start(bf16[48,2048]{1,0:T(8,128)(2,1)S(1)} %get-tuple-element.243), channel_id=1, source_target_pairs={{0,8},{1,9},{2,10},{3,11},{4,12},{5,13},{6,14},{7,15},{8,0},{9,1},... | collective-permute-start | bytes 589832 | tf_op jit(solution)/shard_map/ppermute | solution.py:398
  134.9 2.9 %collective-permute-done.32.swapped = bf16[2,256,512]{2,1,0:T(8,128)(2,1)S(1)} collective-permute-done((bf16[2,256,512]{2,1,0:T(8,128)(2,1)S(1)}, bf16[2,256,512]{2,1,0:T(8,128)(2,1)S(1)}, u32[]{:S(2)}, u32[]{:S(2)}) %collective-permute-start.32) | collective-permute-done | bytes 524320 | tf_op jit(solution)/shard_map/ppermute | solution.py:398
  144.8 3.2 %collective-permute-start.40 = (bf16[256,512]{1,0:T(8,128)(2,1)S(1)}, bf16[256,512]{1,0:T(8,128)(2,1)S(1)}, u32[]{:S(2)}, u32[]{:S(2)}) collective-permute-start(bf16[256,512]{1,0:T(8,128)(2,1)S(1)} %get-tuple-element.289.refs_0_), channel_id=1, source_target_pairs={{0,2},{1,3},{2,0},{3,1},{4,6},{5,7},{6,4},{7,5},{8,10},{9,11},{10,... | collective-permute-start | bytes 786440 | tf_op jit(solution)/shard_map/ppermute | solution.py:604
  150.8 4.3 %collective-permute-done.40.refs_0_ = bf16[256,512]{1,0:T(8,128)(2,1)S(1)} collective-permute-done((bf16[256,512]{1,0:T(8,128)(2,1)S(1)}, bf16[256,512]{1,0:T(8,128)(2,1)S(1)}, u32[]{:S(2)}, u32[]{:S(2)}) %collective-permute-start.40) | collective-permute-done | bytes 262176 | tf_op jit(solution)/shard_map/ppermute | solution.py:604
  157.5 3.2 %collective-permute-done.34.refs_0_ = bf16[256,512]{1,0:T(8,128)(2,1)S(1)} collective-permute-done((bf16[256,512]{1,0:T(8,128)(2,1)S(1)}, bf16[256,512]{1,0:T(8,128)(2,1)S(1)}, u32[]{:S(2)}, u32[]{:S(2)}) %collective-permute-start.34) | collective-permute-done | bytes 262176 | tf_op jit(solution)/shard_map/ppermute | solution.py:604
  163.1 3.2 %collective-permute-done.46.refs_0_ = bf16[256,512]{1,0:T(8,128)(2,1)S(1)} collective-permute-done((bf16[256,512]{1,0:T(8,128)(2,1)S(1)}, bf16[256,512]{1,0:T(8,128)(2,1)S(1)}, u32[]{:S(2)}, u32[]{:S(2)}) %collective-permute-start.46) | collective-permute-done | bytes 262176 | tf_op jit(solution)/shard_map/ppermute | solution.py:604
  166.6 3.7 %collective-permute-start.47 = (bf16[256,512]{1,0:T(8,128)(2,1)S(1)}, bf16[256,512]{1,0:T(8,128)(2,1)S(1)}, u32[]{:S(2)}, u32[]{:S(2)}) collective-permute-start(bf16[256,512]{1,0:T(8,128)(2,1)S(1)} %get-tuple-element.296), channel_id=1, source_target_pairs={{0,2},{1,3},{2,0},{3,1},{4,6},{5,7},{6,4},{7,5},{8,10},{9,11},{10,... | collective-permute-start | bytes 786440 | tf_op jit(solution)/shard_map/ppermute | solution.py:604
  172.3 3.7 %collective-permute-start.43 = (bf16[256,512]{1,0:T(8,128)(2,1)S(1)}, bf16[256,512]{1,0:T(8,128)(2,1)S(1)}, u32[]{:S(2)}, u32[]{:S(2)}) collective-permute-start(bf16[256,512]{1,0:T(8,128)(2,1)S(1)} %get-tuple-element.292), channel_id=1, source_target_pairs={{0,2},{1,3},{2,0},{3,1},{4,6},{5,7},{6,4},{7,5},{8,10},{9,11},{10,... | collective-permute-start | bytes 786440 | tf_op jit(solution)/shard_map/ppermute | solution.py:604
  177.9 3.7 %collective-permute-start.37 = (bf16[256,512]{1,0:T(8,128)(2,1)S(1)}, bf16[256,512]{1,0:T(8,128)(2,1)S(1)}, u32[]{:S(2)}, u32[]{:S(2)}) collective-permute-start(bf16[256,512]{1,0:T(8,128)(2,1)S(1)} %get-tuple-element.285), channel_id=1, source_target_pairs={{0,2},{1,3},{2,0},{3,1},{4,6},{5,7},{6,4},{7,5},{8,10},{9,11},{10,... | collective-permute-start | bytes 786440 | tf_op jit(solution)/shard_map/ppermute | solution.py:604
  183.5 3.7 %collective-permute-start.49 = (bf16[256,512]{1,0:T(8,128)(2,1)S(1)}, bf16[256,512]{1,0:T(8,128)(2,1)S(1)}, u32[]{:S(2)}, u32[]{:S(2)}) collective-permute-start(bf16[256,512]{1,0:T(8,128)(2,1)S(1)} %get-tuple-element.298), channel_id=1, source_target_pairs={{0,2},{1,3},{2,0},{3,1},{4,6},{5,7},{6,4},{7,5},{8,10},{9,11},{10,... | collective-permute-start | bytes 786440 | tf_op jit(solution)/shard_map/ppermute | solution.py:604
  191.2 3.2 %collective-permute-done.37.refs_0_ = bf16[256,512]{1,0:T(8,128)(2,1)S(1)} collective-permute-done((bf16[256,512]{1,0:T(8,128)(2,1)S(1)}, bf16[256,512]{1,0:T(8,128)(2,1)S(1)}, u32[]{:S(2)}, u32[]{:S(2)}) %collective-permute-start.37) | collective-permute-done | bytes 262176 | tf_op jit(solution)/shard_map/ppermute | solution.py:604
  195.4 4.1 %collective-permute-done.49.refs_0_ = bf16[256,512]{1,0:T(8,128)(2,1)S(1)} collective-permute-done((bf16[256,512]{1,0:T(8,128)(2,1)S(1)}, bf16[256,512]{1,0:T(8,128)(2,1)S(1)}, u32[]{:S(2)}, u32[]{:S(2)}) %collective-permute-start.49) | collective-permute-done | bytes 262176 | tf_op jit(solution)/shard_map/ppermute | solution.py:604
  (124 shorter events, 100.2 us)
Async XLA Ops:
  47.4 12.1 %collective-permute-start.13 = (bf16[48,2048]{1,0:T(8,128)(2,1)S(1)}, bf16[48,2048]{1,0:T(8,128)(2,1)S(1)}, u32[]{:S(2)}, u32[]{:S(2)}) collective-permute-start(bf16[48,2048]{1,0:T(8,128)(2,1)S(1)} %get-tuple-element.185), channel_id=1, source_target_pairs={{0,8},{1,9},{2,10},{3,11},{4,12},{5,13},{6,14},{7,15},{8,0},{9,1},... | collective-permute-start | bytes 589832 | tf_op jit(solution)/shard_map/ppermute | solution.py:398
  51.7 11.9 %collective-permute-start.14 = (bf16[48,2048]{1,0:T(8,128)(2,1)S(1)}, bf16[48,2048]{1,0:T(8,128)(2,1)S(1)}, u32[]{:S(2)}, u32[]{:S(2)}) collective-permute-start(bf16[48,2048]{1,0:T(8,128)(2,1)S(1)} %get-tuple-element.186), channel_id=1, source_target_pairs={{0,1},{1,0},{2,3},{3,2},{4,5},{5,4},{6,7},{7,6},{8,16},{9,17},{10,... | collective-permute-start | bytes 589832 | tf_op jit(solution)/shard_map/ppermute | solution.py:398
  51.8 11.9 %collective-permute-start.15 = (bf16[48,2048]{1,0:T(8,128)(2,1)S(1)}, bf16[48,2048]{1,0:T(8,128)(2,1)S(1)}, u32[]{:S(2)}, u32[]{:S(2)}) collective-permute-start(bf16[48,2048]{1,0:T(8,128)(2,1)S(1)} %get-tuple-element.187), channel_id=1, source_target_pairs={{0,1},{1,0},{2,3},{3,2},{4,5},{5,4},{6,7},{7,6},{8,9},{9,8},{10,11... | collective-permute-start | bytes 589832 | tf_op jit(solution)/shard_map/ppermute | solution.py:398
  52.2 11.9 %collective-permute-start.16 = (bf16[48,2048]{1,0:T(8,128)(2,1)S(1)}, bf16[48,2048]{1,0:T(8,128)(2,1)S(1)}, u32[]{:S(2)}, u32[]{:S(2)}) collective-permute-start(bf16[48,2048]{1,0:T(8,128)(2,1)S(1)} %get-tuple-element.195), channel_id=1, source_target_pairs={{0,1},{1,0},{2,3},{3,2},{4,5},{5,4},{6,7},{7,6},{8,16},{9,17},{10,... | collective-permute-start | bytes 589832 | tf_op jit(solution)/shard_map/ppermute | solution.py:398
  52.6 19.5 %collective-permute-start.17 = (bf16[48,2048]{1,0:T(8,128)(2,1)S(1)}, bf16[48,2048]{1,0:T(8,128)(2,1)S(1)}, u32[]{:S(2)}, u32[]{:S(2)}) collective-permute-start(bf16[48,2048]{1,0:T(8,128)(2,1)S(1)} %get-tuple-element.196), channel_id=1, source_target_pairs={{0,1},{1,0},{2,3},{3,2},{4,5},{5,4},{6,7},{7,6},{8,9},{9,8},{10,11... | collective-permute-start | bytes 589832 | tf_op jit(solution)/shard_map/ppermute | solution.py:398
  59.4 13.0 %collective-permute-start.18 = (bf16[48,2048]{1,0:T(8,128)(2,1)S(1)}, bf16[48,2048]{1,0:T(8,128)(2,1)S(1)}, u32[]{:S(2)}, u32[]{:S(2)}) collective-permute-start(bf16[48,2048]{1,0:T(8,128)(2,1)S(1)} %get-tuple-element.197), channel_id=1, source_target_pairs={{0,8},{1,9},{2,10},{3,11},{4,12},{5,13},{6,14},{7,15},{8,0},{9,1},... | collective-permute-start | bytes 589832 | tf_op jit(solution)/shard_map/ppermute | solution.py:398
  63.7 16.8 %collective-permute-start.19 = (bf16[48,2048]{1,0:T(8,128)(2,1)S(1)}, bf16[48,2048]{1,0:T(8,128)(2,1)S(1)}, u32[]{:S(2)}, u32[]{:S(2)}) collective-permute-start(bf16[48,2048]{1,0:T(8,128)(2,1)S(1)} %get-tuple-element.205), channel_id=1, source_target_pairs={{0,1},{1,0},{2,3},{3,2},{4,5},{5,4},{6,7},{7,6},{8,16},{9,17},{10,... | collective-permute-start | bytes 589832 | tf_op jit(solution)/shard_map/ppermute | solution.py:398
  63.9 16.6 %collective-permute-start.20 = (bf16[48,2048]{1,0:T(8,128)(2,1)S(1)}, bf16[48,2048]{1,0:T(8,128)(2,1)S(1)}, u32[]{:S(2)}, u32[]{:S(2)}) collective-permute-start(bf16[48,2048]{1,0:T(8,128)(2,1)S(1)} %get-tuple-element.206), channel_id=1, source_target_pairs={{0,1},{1,0},{2,3},{3,2},{4,5},{5,4},{6,7},{7,6},{8,9},{9,8},{10,11... | collective-permute-start | bytes 589832 | tf_op jit(solution)/shard_map/ppermute | solution.py:398
  64.2 17.7 %collective-permute-start.21 = (bf16[48,2048]{1,0:T(8,128)(2,1)S(1)}, bf16[48,2048]{1,0:T(8,128)(2,1)S(1)}, u32[]{:S(2)}, u32[]{:S(2)}) collective-permute-start(bf16[48,2048]{1,0:T(8,128)(2,1)S(1)} %get-tuple-element.207), channel_id=1, source_target_pairs={{0,8},{1,9},{2,10},{3,11},{4,12},{5,13},{6,14},{7,15},{8,0},{9,1},... | collective-permute-start | bytes 589832 | tf_op jit(solution)/shard_map/ppermute | solution.py:398
  74.8 14.1 %collective-permute-start.22 = (bf16[48,2048]{1,0:T(8,128)(2,1)S(1)}, bf16[48,2048]{1,0:T(8,128)(2,1)S(1)}, u32[]{:S(2)}, u32[]{:S(2)}) collective-permute-start(bf16[48,2048]{1,0:T(8,128)(2,1)S(1)} %get-tuple-element.215), channel_id=1, source_target_pairs={{0,1},{1,0},{2,3},{3,2},{4,5},{5,4},{6,7},{7,6},{8,9},{9,8},{10,11... | collective-permute-start | bytes 589832 | tf_op jit(solution)/shard_map/ppermute | solution.py:398
  74.9 14.0 %collective-permute-start.23 = (bf16[48,2048]{1,0:T(8,128)(2,1)S(1)}, bf16[48,2048]{1,0:T(8,128)(2,1)S(1)}, u32[]{:S(2)}, u32[]{:S(2)}) collective-permute-start(bf16[48,2048]{1,0:T(8,128)(2,1)S(1)} %get-tuple-element.216), channel_id=1, source_target_pairs={{0,16},{1,17},{2,18},{3,19},{4,20},{5,21},{6,22},{7,23},{8,0},{9,1... | collective-permute-start | bytes 589832 | tf_op jit(solution)/shard_map/ppermute | solution.py:398
  96.4 13.7 %collective-permute-start.27 = (bf16[48,2048]{1,0:T(8,128)(2,1)S(1)}, bf16[48,2048]{1,0:T(8,128)(2,1)S(1)}, u32[]{:S(2)}, u32[]{:S(2)}) collective-permute-start(bf16[48,2048]{1,0:T(8,128)(2,1)S(1)} %get-tuple-element.232), channel_id=1, source_target_pairs={{0,24},{1,25},{2,26},{3,27},{4,28},{5,29},{6,30},{7,31},{8,0},{9,1... | collective-permute-start | bytes 589832 | tf_op jit(solution)/shard_map/ppermute | solution.py:398
  144.3 22.0 %collective-permute-start.45 = (bf16[4,256,512]{2,1,0:T(8,128)(2,1)S(1)}, bf16[4,256,512]{2,1,0:T(8,128)(2,1)S(1)}, u32[]{:S(2)}, u32[]{:S(2)}) collective-permute-start(bf16[4,256,512]{2,1,0:T(8,128)(2,1)S(1)} %get-tuple-element.295), channel_id=1, source_target_pairs={{0,1},{1,0},{2,3},{3,2},{4,5},{5,4},{6,7},{7,6},{8,9},{9,8},{10,11... | collective-permute-start | bytes 3145736 | tf_op jit(solution)/shard_map/ppermute | solution.py:398
  148.8 11.9 %collective-permute-start.34 = (bf16[256,512]{1,0:T(8,128)(2,1)S(1)}, bf16[256,512]{1,0:T(8,128)(2,1)S(1)}, u32[]{:S(2)}, u32[]{:S(2)}) collective-permute-start(bf16[256,512]{1,0:T(8,128)(2,1)S(1)} %get-tuple-element.282), channel_id=1, source_target_pairs={{0,2},{1,3},{2,0},{3,1},{4,6},{5,7},{6,4},{7,5},{8,10},{9,11},{10,... | collective-permute-start | bytes 786440 | tf_op jit(solution)/shard_map/ppermute | solution.py:604
  148.8 17.5 %collective-permute-start.46 = (bf16[256,512]{1,0:T(8,128)(2,1)S(1)}, bf16[256,512]{1,0:T(8,128)(2,1)S(1)}, u32[]{:S(2)}, u32[]{:S(2)}) collective-permute-start(bf16[256,512]{1,0:T(8,128)(2,1)S(1)} %get-tuple-element.279.refs_0_), channel_id=1, source_target_pairs={{0,2},{1,3},{2,0},{3,1},{4,6},{5,7},{6,4},{7,5},{8,10},{9,11},{10,... | collective-permute-start | bytes 786440 | tf_op jit(solution)/shard_map/ppermute | solution.py:604
  155.4 16.6 %collective-permute-start.41 = (bf16[256,512]{1,0:T(8,128)(2,1)S(1)}, bf16[256,512]{1,0:T(8,128)(2,1)S(1)}, u32[]{:S(2)}, u32[]{:S(2)}) collective-permute-start(bf16[256,512]{1,0:T(8,128)(2,1)S(1)} %get-tuple-element.290), channel_id=1, source_target_pairs={{0,2},{1,3},{2,0},{3,1},{4,6},{5,7},{6,4},{7,5},{8,10},{9,11},{10,... | collective-permute-start | bytes 786440 | tf_op jit(solution)/shard_map/ppermute | solution.py:604
  157.5 14.5 %collective-permute-start.42 = (bf16[256,512]{1,0:T(8,128)(2,1)S(1)}, bf16[256,512]{1,0:T(8,128)(2,1)S(1)}, u32[]{:S(2)}, u32[]{:S(2)}) collective-permute-start(bf16[256,512]{1,0:T(8,128)(2,1)S(1)} %get-tuple-element.291), channel_id=1, source_target_pairs={{0,1},{1,0},{2,4},{3,5},{4,2},{5,3},{6,7},{7,6},{8,9},{9,8},{10,12... | collective-permute-start | bytes 786440 | tf_op jit(solution)/shard_map/ppermute | solution.py:604
  161.0 16.6 %collective-permute-start.35 = (bf16[256,512]{1,0:T(8,128)(2,1)S(1)}, bf16[256,512]{1,0:T(8,128)(2,1)S(1)}, u32[]{:S(2)}, u32[]{:S(2)}) collective-permute-start(bf16[256,512]{1,0:T(8,128)(2,1)S(1)} %get-tuple-element.283), channel_id=1, source_target_pairs={{0,2},{1,3},{2,0},{3,1},{4,6},{5,7},{6,4},{7,5},{8,10},{9,11},{10,... | collective-permute-start | bytes 786440 | tf_op jit(solution)/shard_map/ppermute | solution.py:604
  166.3 11.2 %collective-permute-start.36 = (bf16[256,512]{1,0:T(8,128)(2,1)S(1)}, bf16[256,512]{1,0:T(8,128)(2,1)S(1)}, u32[]{:S(2)}, u32[]{:S(2)}) collective-permute-start(bf16[256,512]{1,0:T(8,128)(2,1)S(1)} %get-tuple-element.284), channel_id=1, source_target_pairs={{0,1},{1,0},{2,4},{3,5},{4,2},{5,3},{6,7},{7,6},{8,9},{9,8},{10,12... | collective-permute-start | bytes 786440 | tf_op jit(solution)/shard_map/ppermute | solution.py:604
  166.6 16.5 %collective-permute-start.47 = (bf16[256,512]{1,0:T(8,128)(2,1)S(1)}, bf16[256,512]{1,0:T(8,128)(2,1)S(1)}, u32[]{:S(2)}, u32[]{:S(2)}) collective-permute-start(bf16[256,512]{1,0:T(8,128)(2,1)S(1)} %get-tuple-element.296), channel_id=1, source_target_pairs={{0,2},{1,3},{2,0},{3,1},{4,6},{5,7},{6,4},{7,5},{8,10},{9,11},{10,... | collective-permute-start | bytes 786440 | tf_op jit(solution)/shard_map/ppermute | solution.py:604
  172.3 16.5 %collective-permute-start.43 = (bf16[256,512]{1,0:T(8,128)(2,1)S(1)}, bf16[256,512]{1,0:T(8,128)(2,1)S(1)}, u32[]{:S(2)}, u32[]{:S(2)}) collective-permute-start(bf16[256,512]{1,0:T(8,128)(2,1)S(1)} %get-tuple-element.292), channel_id=1, source_target_pairs={{0,2},{1,3},{2,0},{3,1},{4,6},{5,7},{6,4},{7,5},{8,10},{9,11},{10,... | collective-permute-start | bytes 786440 | tf_op jit(solution)/shard_map/ppermute | solution.py:604
  177.5 12.7 %collective-permute-start.44 = (bf16[256,512]{1,0:T(8,128)(2,1)S(1)}, bf16[256,512]{1,0:T(8,128)(2,1)S(1)}, u32[]{:S(2)}, u32[]{:S(2)}) collective-permute-start(bf16[256,512]{1,0:T(8,128)(2,1)S(1)} %get-tuple-element.293), channel_id=1, source_target_pairs={{0,1},{1,0},{2,4},{3,5},{4,2},{5,3},{6,7},{7,6},{8,9},{9,8},{10,12... | collective-permute-start | bytes 786440 | tf_op jit(solution)/shard_map/ppermute | solution.py:604
  177.9 16.5 %collective-permute-start.37 = (bf16[256,512]{1,0:T(8,128)(2,1)S(1)}, bf16[256,512]{1,0:T(8,128)(2,1)S(1)}, u32[]{:S(2)}, u32[]{:S(2)}) collective-permute-start(bf16[256,512]{1,0:T(8,128)(2,1)S(1)} %get-tuple-element.285), channel_id=1, source_target_pairs={{0,2},{1,3},{2,0},{3,1},{4,6},{5,7},{6,4},{7,5},{8,10},{9,11},{10,... | collective-permute-start | bytes 786440 | tf_op jit(solution)/shard_map/ppermute | solution.py:604
  183.5 15.9 %collective-permute-start.49 = (bf16[256,512]{1,0:T(8,128)(2,1)S(1)}, bf16[256,512]{1,0:T(8,128)(2,1)S(1)}, u32[]{:S(2)}, u32[]{:S(2)}) collective-permute-start(bf16[256,512]{1,0:T(8,128)(2,1)S(1)} %get-tuple-element.298), channel_id=1, source_target_pairs={{0,2},{1,3},{2,0},{3,1},{4,6},{5,7},{6,4},{7,5},{8,10},{9,11},{10,... | collective-permute-start | bytes 786440 | tf_op jit(solution)/shard_map/ppermute | solution.py:604
  (29 other events, 218.3 us)

commit v2 on v1

--- a/solution.py
+++ b/solution.py
@@ -68,7 +68,7 @@
 
 
 def tick_kernel(tick, micro, rows, sections, plan, *refs):
-    runs_f, runs_b, routes, arrivals, places, inputs, starts_f, starts_b, loading = plan
+    runs_f, runs_b, routes, arrivals, places, inputs, starts_f, starts_b, loading, defer = plan
     refs = list(refs)
     place = lax.axis_index("section")
     tokens = refs.pop(0) if inputs[0] else None
@@ -228,11 +228,13 @@
                 )
                 wide[:, columns] = d_norm
 
-            pieces(x_b.shape[1], PIECES_B, exit_)
             xf = x_b[...].astype(f32)
             scale = lax.rsqrt(jnp.mean(xf * xf, axis=-1, keepdims=True) + 1e-06)
             x_hat = xf * scale
             norms[...] = x_hat.astype(bf16)
+            if defer:
+                return
+            pieces(x_b.shape[1], PIECES_B, exit_)
             d_norm = wide[...]
             inner = jnp.mean(d_norm * x_hat, axis=-1, keepdims=True)
             grad = grad_in[...].astype(f32) + scale * (d_norm - x_hat * inner)
@@ -274,6 +276,7 @@
         starts_f,
         starts_b,
         loading,
+        tick == micro + starts_b[0] - 1,
     )
     result = pl.pallas_call(
         functools.partial(tick_kernel, tick, micro, rows, sections, plan),
@@ -307,6 +310,46 @@
     kept = rest[:3] if runs_f else None
     terms = rest[-3:] if runs_b else None
     return outs, kept, terms, loaded
+
+
+def tail_kernel(grad_in, x, terms, w_gate, w_up, after, out, wide):
+    units = w_gate.shape[1]
+
+    @pl.when(lax.axis_index("section") == 0)
+    def work():
+        def exit_(columns):
+            d_norm = lax.dot_general(
+                terms[:, pl.ds(2 * units, units)], w_gate[columns, :], NT, preferred_element_type=f32
+            )
+            wide[:, columns] = d_norm + lax.dot_general(
+                terms[:, pl.ds(units, units)], w_up[columns, :], NT, preferred_element_type=f32
+            )
+
+        pieces(x.shape[1], PIECES_B, exit_)
+        xf = x[...].astype(f32)
+        scale = lax.rsqrt(jnp.mean(xf * xf, axis=-1, keepdims=True) + 1e-06)
+        x_hat = xf * scale
+        d_norm = wide[...]
+        inner = jnp.mean(d_norm * x_hat, axis=-1, keepdims=True)
+        grad = grad_in[...].astype(f32) + scale * (d_norm - x_hat * inner)
+        out[...] = grad.astype(bf16)
+
+
+def tail_call(grad_in, x, terms, w_gate, w_up, after):
+    rows, width = x.shape
+    units = w_gate.shape[1]
+    return pl.pallas_call(
+        tail_kernel,
+        out_shape=shape_of(rows, width),
+        in_specs=[VM] * 5 + [ANY],
+        out_specs=VM,
+        scratch_shapes=[pltpu.VMEM((rows, width), f32)],
+        compiler_params=pltpu.CompilerParams(vmem_limit_bytes=10 << 20),
+        cost_estimate=pl.CostEstimate(
+            flops=4 * rows * width * units, bytes_accessed=4 * width * units, transcendentals=0
+        ),
+        name="tail",
+    )(grad_in, x, terms, w_gate, w_up, after)
 
 
 def collect_call(micro, rows, sections, total, whole, sources):
@@ -561,7 +604,9 @@
 
     laid = functools.partial(collect_call, micro, rows, sections, total)
     all_in = collect_call(micro, rows, sections, total, arrays[1], arrivals)
-    all_grad, normed, terms = [laid(None, list(column)) for column in zip(*history)]
+    grads, norms, terms = [list(column) for column in zip(*history)]
+    last_terms = terms[-1]
+    normed, terms = laid(None, norms), laid(None, terms)
     near = [(z, z ^ 1) for z in range(chips)]
     far = [(z, ((z + 1) ^ 1) - 1) for z in range(chips)]
     held = {}
@@ -588,6 +633,8 @@
     out, moving[1] = advance(1, 1, [])
     begin(0, [out])
     moving[2] = advance(1, 2, [])[1]
+    grads[-1] = tail_call(arrivals[-1][0], kept[micro - 1][2], last_terms, *arrays[2:4], out)
+    all_grad = laid(None, grads)
     for step in range(2, chips):
         for which in range(3):
             moving[which] = advance(step, which, moving[which])[1]

time: 201 us -> 200 us (level)
  transfers between devices with their start and end apart: 51 -> 51, of which waited for: 23 -> 23; matrix products, arithmetic and copies ran while one was open for 0% -> 0% of each run, Pallas kernels for 27% -> 28%
where the time goes in v2:
time: 200 us
  starting transfers between devices  85.6 us (43%)
  Pallas kernels  66.8 us (33%)
  waiting for transfers between devices  44.9 us (22%)
    ppermute x36, starting transfers between devices, permute(): return lax.ppermute(value, ('section', 'dp'), pairs)  61.5 us
    pallas_call x22, Pallas kernels, tick_call(): pl.pallas_call(functools.partial(tick_kernel, tick, micro, rows, sections...  47.5 us
    ppermute x15, starting transfers between devices, line(): return lax.ppermute(value, 'dp', route)  24.1 us
    ppermute x15, waiting for transfers between devices, line(): return lax.ppermute(value, 'dp', route)  22.6 us
    ppermute x36, waiting for transfers between devices, permute(): return lax.ppermute(value, ('section', 'dp'), pairs)  22.3 us
    pallas_call x4, Pallas kernels, weight_call(): pl.pallas_call(weight_kernel, out_shape=[shape_of(count, half, units)] *...  8.26 us
    pallas_call x9, Pallas kernels, step_call(): pl.pallas_call(functools.partial(step_kernel, step, chips), out_shape=[sh...  4.47 us
  transfers between devices with their start and end apart: 51, of which 23 were waited for; matrix products, arithmetic and copies ran while one was open for 0% of the time, Pallas kernels for 28%

profile of v2, /device:TPU:0, one launch (start us, length us, event | category | flops | bytes accessed | tf_op | source)
XLA Modules:
  0.0 199.8 jit_solution(3040154653890656146)
XLA Ops:
  2.2 4.3 %tick.22 = (bf16[48,2048]{1,0:T(8,128)(2,1)S(1)}, f32[48,512]{1,0:T(8,128)S(1)}, f32[48,512]{1,0:T(8,128)S(1)}, bf16[48,2048]{1,0:T(8,128)(2,1)S(1)}, bf16[2048,...) custom-call(bf16[480,2048]{1,0:T(8,128)(2,1)S(1)} %copy-done.1, ...), custom_call_target="tpu_custom_call" | custom-call | flops 301989888 | bytes 6291456 | tf_op jit(solution)/shard_map/tick/pallas_call | solution.py:281
  10.4 3.9 %collective-permute-done.refs_4_ = bf16[48,2048]{1,0:T(8,128)(2,1)S(1)} collective-permute-done((bf16[48,2048]{1,0:T(8,128)(2,1)S(1)}, bf16[48,2048]{1,0:T(8,128)(2,1)S(1)}, u32[]{:S(2)}, u32[]{:S(2)}) %collective-permute-start) | collective-permute-done | bytes 196640 | tf_op jit(solution)/shard_map/ppermute | solution.py:441
  47.4 4.4 %collective-permute-start.13 = (bf16[48,2048]{1,0:T(8,128)(2,1)S(1)}, bf16[48,2048]{1,0:T(8,128)(2,1)S(1)}, u32[]{:S(2)}, u32[]{:S(2)}) collective-permute-start(bf16[48,2048]{1,0:T(8,128)(2,1)S(1)} %get-tuple-element.184), channel_id=1, source_target_pairs={{0,8},{1,9},{2,10},{3,11},{4,12},{5,13},{6,14},{7,15},{8,0},{9,1},... | collective-permute-start | bytes 589832 | tf_op jit(solution)/shard_map/ppermute | solution.py:441
  52.9 6.6 %collective-permute-done.13.refs_4_ = bf16[48,2048]{1,0:T(8,128)(2,1)S(1)} collective-permute-done((bf16[48,2048]{1,0:T(8,128)(2,1)S(1)}, bf16[48,2048]{1,0:T(8,128)(2,1)S(1)}, u32[]{:S(2)}, u32[]{:S(2)}) %collective-permute-start.13) | collective-permute-done | bytes 196640 | tf_op jit(solution)/shard_map/ppermute | solution.py:441
  59.5 4.3 %collective-permute-start.18 = (bf16[48,2048]{1,0:T(8,128)(2,1)S(1)}, bf16[48,2048]{1,0:T(8,128)(2,1)S(1)}, u32[]{:S(2)}, u32[]{:S(2)}) collective-permute-start(bf16[48,2048]{1,0:T(8,128)(2,1)S(1)} %get-tuple-element.196), channel_id=1, source_target_pairs={{0,8},{1,9},{2,10},{3,11},{4,12},{5,13},{6,14},{7,15},{8,0},{9,1},... | collective-permute-start | bytes 589832 | tf_op jit(solution)/shard_map/ppermute | solution.py:441
  64.3 7.8 %collective-permute-start.21 = (bf16[48,2048]{1,0:T(8,128)(2,1)S(1)}, bf16[48,2048]{1,0:T(8,128)(2,1)S(1)}, u32[]{:S(2)}, u32[]{:S(2)}) collective-permute-start(bf16[48,2048]{1,0:T(8,128)(2,1)S(1)} %get-tuple-element.206), channel_id=1, source_target_pairs={{0,8},{1,9},{2,10},{3,11},{4,12},{5,13},{6,14},{7,15},{8,0},{9,1},... | collective-permute-start | bytes 589832 | tf_op jit(solution)/shard_map/ppermute | solution.py:441
  75.1 5.5 %collective-permute-start.23 = (bf16[48,2048]{1,0:T(8,128)(2,1)S(1)}, bf16[48,2048]{1,0:T(8,128)(2,1)S(1)}, u32[]{:S(2)}, u32[]{:S(2)}) collective-permute-start(bf16[48,2048]{1,0:T(8,128)(2,1)S(1)} %get-tuple-element.215), channel_id=1, source_target_pairs={{0,16},{1,17},{2,18},{3,19},{4,20},{5,21},{6,22},{7,23},{8,0},{9,1... | collective-permute-start | bytes 589832 | tf_op jit(solution)/shard_map/ppermute | solution.py:441
  84.5 4.5 %collective-permute-start.25 = (bf16[48,2048]{1,0:T(8,128)(2,1)S(1)}, bf16[48,2048]{1,0:T(8,128)(2,1)S(1)}, u32[]{:S(2)}, u32[]{:S(2)}) collective-permute-start(bf16[48,2048]{1,0:T(8,128)(2,1)S(1)} %get-tuple-element.221), channel_id=1, source_target_pairs={{0,16},{1,17},{2,18},{3,19},{4,20},{5,21},{6,22},{7,23},{8,0},{9,1... | collective-permute-start | bytes 589832 | tf_op jit(solution)/shard_map/ppermute | solution.py:441
  89.0 3.2 %tick.36 = (bf16[48,2048]{1,0:T(8,128)(2,1)S(1)}, f32[48,512]{1,0:T(8,128)}, f32[48,512]{1,0:T(8,128)}, bf16[48,2048]{1,0:T(8,128)(2,1)}, bf16[48,2048]{1,0:T(8,...) custom-call(bf16[480,2048]{1,0:T(8,128)(2,1)S(1)} %copy-done, ...), custom_call_target="tpu_custom_call" | custom-call | flops 603979776 | bytes 6291456 | tf_op jit(solution)/shard_map/tick/pallas_call | solution.py:281
  93.3 3.2 %tick.37 = (bf16[48,2048]{1,0:T(8,128)(2,1)S(1)}, f32[48,512]{1,0:T(8,128)}, f32[48,512]{1,0:T(8,128)}, bf16[48,2048]{1,0:T(8,128)(2,1)}, bf16[48,2048]{1,0:T(8,...) custom-call(bf16[480,2048]{1,0:T(8,128)(2,1)S(1)} %copy-done, ...), custom_call_target="tpu_custom_call" | custom-call | flops 603979776 | bytes 6291456 | tf_op jit(solution)/shard_map/tick/pallas_call | solution.py:281
  96.5 5.2 %collective-permute-start.27 = (bf16[48,2048]{1,0:T(8,128)(2,1)S(1)}, bf16[48,2048]{1,0:T(8,128)(2,1)S(1)}, u32[]{:S(2)}, u32[]{:S(2)}) collective-permute-start(bf16[48,2048]{1,0:T(8,128)(2,1)S(1)} %get-tuple-element.231), channel_id=1, source_target_pairs={{0,24},{1,25},{2,26},{3,27},{4,28},{5,29},{6,30},{7,31},{8,0},{9,1... | collective-permute-start | bytes 589832 | tf_op jit(solution)/shard_map/ppermute | solution.py:441
  104.2 4.6 %collective-permute-start.28 = (bf16[48,2048]{1,0:T(8,128)(2,1)S(1)}, bf16[48,2048]{1,0:T(8,128)(2,1)S(1)}, u32[]{:S(2)}, u32[]{:S(2)}) collective-permute-start(bf16[48,2048]{1,0:T(8,128)(2,1)S(1)} %get-tuple-element.236), channel_id=1, source_target_pairs={{0,16},{1,17},{2,18},{3,19},{4,20},{5,21},{6,22},{7,23},{8,0},{9,1... | collective-permute-start | bytes 589832 | tf_op jit(solution)/shard_map/ppermute | solution.py:441
  116.1 2.7 %collective-permute-start.30 = (bf16[48,2048]{1,0:T(8,128)(2,1)S(1)}, bf16[48,2048]{1,0:T(8,128)(2,1)S(1)}, u32[]{:S(2)}, u32[]{:S(2)}) collective-permute-start(bf16[48,2048]{1,0:T(8,128)(2,1)S(1)} %get-tuple-element.240), channel_id=1, source_target_pairs={{0,8},{1,9},{2,10},{3,11},{4,12},{5,13},{6,14},{7,15},{8,0},{9,1},... | collective-permute-start | bytes 589832 | tf_op jit(solution)/shard_map/ppermute | solution.py:441
  121.4 3.0 %collective-permute-start.31 = (bf16[48,2048]{1,0:T(8,128)(2,1)S(1)}, bf16[48,2048]{1,0:T(8,128)(2,1)S(1)}, u32[]{:S(2)}, u32[]{:S(2)}) collective-permute-start(bf16[48,2048]{1,0:T(8,128)(2,1)S(1)} %get-tuple-element.242), channel_id=1, source_target_pairs={{0,8},{1,9},{2,10},{3,11},{4,12},{5,13},{6,14},{7,15},{8,0},{9,1},... | collective-permute-start | bytes 589832 | tf_op jit(solution)/shard_map/ppermute | solution.py:441
  134.1 2.9 %collective-permute-done.33.swapped = bf16[2,256,512]{2,1,0:T(8,128)(2,1)S(1)} collective-permute-done((bf16[2,256,512]{2,1,0:T(8,128)(2,1)S(1)}, bf16[2,256,512]{2,1,0:T(8,128)(2,1)S(1)}, u32[]{:S(2)}, u32[]{:S(2)}) %collective-permute-start.33) | collective-permute-done | bytes 524320 | tf_op jit(solution)/shard_map/ppermute | solution.py:441
  144.0 3.2 %collective-permute-start.40 = (bf16[256,512]{1,0:T(8,128)(2,1)S(1)}, bf16[256,512]{1,0:T(8,128)(2,1)S(1)}, u32[]{:S(2)}, u32[]{:S(2)}) collective-permute-start(bf16[256,512]{1,0:T(8,128)(2,1)S(1)} %get-tuple-element.278.after.refs_0_), channel_id=1, source_target_pairs={{0,2},{1,3},{2,0},{3,1},{4,6},{5,7},{6,4},{7,5},{8,10},{9,11},{10,... | collective-permute-start | bytes 786440 | tf_op jit(solution)/shard_map/ppermute | solution.py:651
  150.1 4.3 %collective-permute-done.40.refs_0_ = bf16[256,512]{1,0:T(8,128)(2,1)S(1)} collective-permute-done((bf16[256,512]{1,0:T(8,128)(2,1)S(1)}, bf16[256,512]{1,0:T(8,128)(2,1)S(1)}, u32[]{:S(2)}, u32[]{:S(2)}) %collective-permute-start.40) | collective-permute-done | bytes 262176 | tf_op jit(solution)/shard_map/ppermute | solution.py:651
  156.8 3.2 %collective-permute-done.35.refs_0_ = bf16[256,512]{1,0:T(8,128)(2,1)S(1)} collective-permute-done((bf16[256,512]{1,0:T(8,128)(2,1)S(1)}, bf16[256,512]{1,0:T(8,128)(2,1)S(1)}, u32[]{:S(2)}, u32[]{:S(2)}) %collective-permute-start.35) | collective-permute-done | bytes 262176 | tf_op jit(solution)/shard_map/ppermute | solution.py:651
  162.4 3.2 %collective-permute-done.46.refs_0_ = bf16[256,512]{1,0:T(8,128)(2,1)S(1)} collective-permute-done((bf16[256,512]{1,0:T(8,128)(2,1)S(1)}, bf16[256,512]{1,0:T(8,128)(2,1)S(1)}, u32[]{:S(2)}, u32[]{:S(2)}) %collective-permute-start.46) | collective-permute-done | bytes 262176 | tf_op jit(solution)/shard_map/ppermute | solution.py:651
  166.0 3.7 %collective-permute-start.47 = (bf16[256,512]{1,0:T(8,128)(2,1)S(1)}, bf16[256,512]{1,0:T(8,128)(2,1)S(1)}, u32[]{:S(2)}, u32[]{:S(2)}) collective-permute-start(bf16[256,512]{1,0:T(8,128)(2,1)S(1)} %get-tuple-element.294), channel_id=1, source_target_pairs={{0,2},{1,3},{2,0},{3,1},{4,6},{5,7},{6,4},{7,5},{8,10},{9,11},{10,... | collective-permute-start | bytes 786440 | tf_op jit(solution)/shard_map/ppermute | solution.py:651
  171.6 3.7 %collective-permute-start.43 = (bf16[256,512]{1,0:T(8,128)(2,1)S(1)}, bf16[256,512]{1,0:T(8,128)(2,1)S(1)}, u32[]{:S(2)}, u32[]{:S(2)}) collective-permute-start(bf16[256,512]{1,0:T(8,128)(2,1)S(1)} %get-tuple-element.290), channel_id=1, source_target_pairs={{0,2},{1,3},{2,0},{3,1},{4,6},{5,7},{6,4},{7,5},{8,10},{9,11},{10,... | collective-permute-start | bytes 786440 | tf_op jit(solution)/shard_map/ppermute | solution.py:651
  177.2 3.7 %collective-permute-start.38 = (bf16[256,512]{1,0:T(8,128)(2,1)S(1)}, bf16[256,512]{1,0:T(8,128)(2,1)S(1)}, u32[]{:S(2)}, u32[]{:S(2)}) collective-permute-start(bf16[256,512]{1,0:T(8,128)(2,1)S(1)} %get-tuple-element.286), channel_id=1, source_target_pairs={{0,2},{1,3},{2,0},{3,1},{4,6},{5,7},{6,4},{7,5},{8,10},{9,11},{10,... | collective-permute-start | bytes 786440 | tf_op jit(solution)/shard_map/ppermute | solution.py:651
  182.9 3.7 %collective-permute-start.49 = (bf16[256,512]{1,0:T(8,128)(2,1)S(1)}, bf16[256,512]{1,0:T(8,128)(2,1)S(1)}, u32[]{:S(2)}, u32[]{:S(2)}) collective-permute-start(bf16[256,512]{1,0:T(8,128)(2,1)S(1)} %get-tuple-element.296), channel_id=1, source_target_pairs={{0,2},{1,3},{2,0},{3,1},{4,6},{5,7},{6,4},{7,5},{8,10},{9,11},{10,... | collective-permute-start | bytes 786440 | tf_op jit(solution)/shard_map/ppermute | solution.py:651
  194.7 4.1 %collective-permute-done.49.refs_0_ = bf16[256,512]{1,0:T(8,128)(2,1)S(1)} collective-permute-done((bf16[256,512]{1,0:T(8,128)(2,1)S(1)}, bf16[256,512]{1,0:T(8,128)(2,1)S(1)}, u32[]{:S(2)}, u32[]{:S(2)}) %collective-permute-start.49) | collective-permute-done | bytes 262176 | tf_op jit(solution)/shard_map/ppermute | solution.py:651
  (125 shorter events, 99.9 us)
Async XLA Ops:
  47.4 12.1 %collective-permute-start.13 = (bf16[48,2048]{1,0:T(8,128)(2,1)S(1)}, bf16[48,2048]{1,0:T(8,128)(2,1)S(1)}, u32[]{:S(2)}, u32[]{:S(2)}) collective-permute-start(bf16[48,2048]{1,0:T(8,128)(2,1)S(1)} %get-tuple-element.184), channel_id=1, source_target_pairs={{0,8},{1,9},{2,10},{3,11},{4,12},{5,13},{6,14},{7,15},{8,0},{9,1},... | collective-permute-start | bytes 589832 | tf_op jit(solution)/shard_map/ppermute | solution.py:441
  51.8 12.0 %collective-permute-start.14 = (bf16[48,2048]{1,0:T(8,128)(2,1)S(1)}, bf16[48,2048]{1,0:T(8,128)(2,1)S(1)}, u32[]{:S(2)}, u32[]{:S(2)}) collective-permute-start(bf16[48,2048]{1,0:T(8,128)(2,1)S(1)} %get-tuple-element.185), channel_id=1, source_target_pairs={{0,1},{1,0},{2,3},{3,2},{4,5},{5,4},{6,7},{7,6},{8,16},{9,17},{10,... | collective-permute-start | bytes 589832 | tf_op jit(solution)/shard_map/ppermute | solution.py:441
  51.8 11.9 %collective-permute-start.15 = (bf16[48,2048]{1,0:T(8,128)(2,1)S(1)}, bf16[48,2048]{1,0:T(8,128)(2,1)S(1)}, u32[]{:S(2)}, u32[]{:S(2)}) collective-permute-start(bf16[48,2048]{1,0:T(8,128)(2,1)S(1)} %get-tuple-element.186), channel_id=1, source_target_pairs={{0,1},{1,0},{2,3},{3,2},{4,5},{5,4},{6,7},{7,6},{8,9},{9,8},{10,11... | collective-permute-start | bytes 589832 | tf_op jit(solution)/shard_map/ppermute | solution.py:441
  52.3 12.0 %collective-permute-start.16 = (bf16[48,2048]{1,0:T(8,128)(2,1)S(1)}, bf16[48,2048]{1,0:T(8,128)(2,1)S(1)}, u32[]{:S(2)}, u32[]{:S(2)}) collective-permute-start(bf16[48,2048]{1,0:T(8,128)(2,1)S(1)} %get-tuple-element.194), channel_id=1, source_target_pairs={{0,1},{1,0},{2,3},{3,2},{4,5},{5,4},{6,7},{7,6},{8,16},{9,17},{10,... | collective-permute-start | bytes 589832 | tf_op jit(solution)/shard_map/ppermute | solution.py:441
  52.6 19.5 %collective-permute-start.17 = (bf16[48,2048]{1,0:T(8,128)(2,1)S(1)}, bf16[48,2048]{1,0:T(8,128)(2,1)S(1)}, u32[]{:S(2)}, u32[]{:S(2)}) collective-permute-start(bf16[48,2048]{1,0:T(8,128)(2,1)S(1)} %get-tuple-element.195), channel_id=1, source_target_pairs={{0,1},{1,0},{2,3},{3,2},{4,5},{5,4},{6,7},{7,6},{8,9},{9,8},{10,11... | collective-permute-start | bytes 589832 | tf_op jit(solution)/shard_map/ppermute | solution.py:441
  59.5 13.0 %collective-permute-start.18 = (bf16[48,2048]{1,0:T(8,128)(2,1)S(1)}, bf16[48,2048]{1,0:T(8,128)(2,1)S(1)}, u32[]{:S(2)}, u32[]{:S(2)}) collective-permute-start(bf16[48,2048]{1,0:T(8,128)(2,1)S(1)} %get-tuple-element.196), channel_id=1, source_target_pairs={{0,8},{1,9},{2,10},{3,11},{4,12},{5,13},{6,14},{7,15},{8,0},{9,1},... | collective-permute-start | bytes 589832 | tf_op jit(solution)/shard_map/ppermute | solution.py:441
  63.8 16.8 %collective-permute-start.19 = (bf16[48,2048]{1,0:T(8,128)(2,1)S(1)}, bf16[48,2048]{1,0:T(8,128)(2,1)S(1)}, u32[]{:S(2)}, u32[]{:S(2)}) collective-permute-start(bf16[48,2048]{1,0:T(8,128)(2,1)S(1)} %get-tuple-element.204), channel_id=1, source_target_pairs={{0,1},{1,0},{2,3},{3,2},{4,5},{5,4},{6,7},{7,6},{8,16},{9,17},{10,... | collective-permute-start | bytes 589832 | tf_op jit(solution)/shard_map/ppermute | solution.py:441
  64.0 16.6 %collective-permute-start.20 = (bf16[48,2048]{1,0:T(8,128)(2,1)S(1)}, bf16[48,2048]{1,0:T(8,128)(2,1)S(1)}, u32[]{:S(2)}, u32[]{:S(2)}) collective-permute-start(bf16[48,2048]{1,0:T(8,128)(2,1)S(1)} %get-tuple-element.205), channel_id=1, source_target_pairs={{0,1},{1,0},{2,3},{3,2},{4,5},{5,4},{6,7},{7,6},{8,9},{9,8},{10,11... | collective-permute-start | bytes 589832 | tf_op jit(solution)/shard_map/ppermute | solution.py:441
  64.3 17.7 %collective-permute-start.21 = (bf16[48,2048]{1,0:T(8,128)(2,1)S(1)}, bf16[48,2048]{1,0:T(8,128)(2,1)S(1)}, u32[]{:S(2)}, u32[]{:S(2)}) collective-permute-start(bf16[48,2048]{1,0:T(8,128)(2,1)S(1)} %get-tuple-element.206), channel_id=1, source_target_pairs={{0,8},{1,9},{2,10},{3,11},{4,12},{5,13},{6,14},{7,15},{8,0},{9,1},... | collective-permute-start | bytes 589832 | tf_op jit(solution)/shard_map/ppermute | solution.py:441
  75.0 14.0 %collective-permute-start.22 = (bf16[48,2048]{1,0:T(8,128)(2,1)S(1)}, bf16[48,2048]{1,0:T(8,128)(2,1)S(1)}, u32[]{:S(2)}, u32[]{:S(2)}) collective-permute-start(bf16[48,2048]{1,0:T(8,128)(2,1)S(1)} %get-tuple-element.214), channel_id=1, source_target_pairs={{0,1},{1,0},{2,3},{3,2},{4,5},{5,4},{6,7},{7,6},{8,9},{9,8},{10,11... | collective-permute-start | bytes 589832 | tf_op jit(solution)/shard_map/ppermute | solution.py:441
  75.1 14.0 %collective-permute-start.23 = (bf16[48,2048]{1,0:T(8,128)(2,1)S(1)}, bf16[48,2048]{1,0:T(8,128)(2,1)S(1)}, u32[]{:S(2)}, u32[]{:S(2)}) collective-permute-start(bf16[48,2048]{1,0:T(8,128)(2,1)S(1)} %get-tuple-element.215), channel_id=1, source_target_pairs={{0,16},{1,17},{2,18},{3,19},{4,20},{5,21},{6,22},{7,23},{8,0},{9,1... | collective-permute-start | bytes 589832 | tf_op jit(solution)/shard_map/ppermute | solution.py:441
  96.5 13.6 %collective-permute-start.27 = (bf16[48,2048]{1,0:T(8,128)(2,1)S(1)}, bf16[48,2048]{1,0:T(8,128)(2,1)S(1)}, u32[]{:S(2)}, u32[]{:S(2)}) collective-permute-start(bf16[48,2048]{1,0:T(8,128)(2,1)S(1)} %get-tuple-element.231), channel_id=1, source_target_pairs={{0,24},{1,25},{2,26},{3,27},{4,28},{5,29},{6,30},{7,31},{8,0},{9,1... | collective-permute-start | bytes 589832 | tf_op jit(solution)/shard_map/ppermute | solution.py:441
  143.6 22.0 %collective-permute-start.45 = (bf16[4,256,512]{2,1,0:T(8,128)(2,1)S(1)}, bf16[4,256,512]{2,1,0:T(8,128)(2,1)S(1)}, u32[]{:S(2)}, u32[]{:S(2)}) collective-permute-start(bf16[4,256,512]{2,1,0:T(8,128)(2,1)S(1)} %get-tuple-element.293), channel_id=1, source_target_pairs={{0,1},{1,0},{2,3},{3,2},{4,5},{5,4},{6,7},{7,6},{8,9},{9,8},{10,11... | collective-permute-start | bytes 3145736 | tf_op jit(solution)/shard_map/ppermute | solution.py:441
  148.1 11.9 %collective-permute-start.35 = (bf16[256,512]{1,0:T(8,128)(2,1)S(1)}, bf16[256,512]{1,0:T(8,128)(2,1)S(1)}, u32[]{:S(2)}, u32[]{:S(2)}) collective-permute-start(bf16[256,512]{1,0:T(8,128)(2,1)S(1)} %get-tuple-element.283), channel_id=1, source_target_pairs={{0,2},{1,3},{2,0},{3,1},{4,6},{5,7},{6,4},{7,5},{8,10},{9,11},{10,... | collective-permute-start | bytes 786440 | tf_op jit(solution)/shard_map/ppermute | solution.py:651
  148.1 17.5 %collective-permute-start.46 = (bf16[256,512]{1,0:T(8,128)(2,1)S(1)}, bf16[256,512]{1,0:T(8,128)(2,1)S(1)}, u32[]{:S(2)}, u32[]{:S(2)}) collective-permute-start(bf16[256,512]{1,0:T(8,128)(2,1)S(1)} %get-tuple-element.280.refs_0_), channel_id=1, source_target_pairs={{0,2},{1,3},{2,0},{3,1},{4,6},{5,7},{6,4},{7,5},{8,10},{9,11},{10,... | collective-permute-start | bytes 786440 | tf_op jit(solution)/shard_map/ppermute | solution.py:651
  154.7 16.6 %collective-permute-start.41 = (bf16[256,512]{1,0:T(8,128)(2,1)S(1)}, bf16[256,512]{1,0:T(8,128)(2,1)S(1)}, u32[]{:S(2)}, u32[]{:S(2)}) collective-permute-start(bf16[256,512]{1,0:T(8,128)(2,1)S(1)} %get-tuple-element.288), channel_id=1, source_target_pairs={{0,2},{1,3},{2,0},{3,1},{4,6},{5,7},{6,4},{7,5},{8,10},{9,11},{10,... | collective-permute-start | bytes 786440 | tf_op jit(solution)/shard_map/ppermute | solution.py:651
  156.8 14.5 %collective-permute-start.42 = (bf16[256,512]{1,0:T(8,128)(2,1)S(1)}, bf16[256,512]{1,0:T(8,128)(2,1)S(1)}, u32[]{:S(2)}, u32[]{:S(2)}) collective-permute-start(bf16[256,512]{1,0:T(8,128)(2,1)S(1)} %get-tuple-element.289), channel_id=1, source_target_pairs={{0,1},{1,0},{2,4},{3,5},{4,2},{5,3},{6,7},{7,6},{8,9},{9,8},{10,12... | collective-permute-start | bytes 786440 | tf_op jit(solution)/shard_map/ppermute | solution.py:651
  160.3 16.6 %collective-permute-start.36 = (bf16[256,512]{1,0:T(8,128)(2,1)S(1)}, bf16[256,512]{1,0:T(8,128)(2,1)S(1)}, u32[]{:S(2)}, u32[]{:S(2)}) collective-permute-start(bf16[256,512]{1,0:T(8,128)(2,1)S(1)} %get-tuple-element.284), channel_id=1, source_target_pairs={{0,2},{1,3},{2,0},{3,1},{4,6},{5,7},{6,4},{7,5},{8,10},{9,11},{10,... | collective-permute-start | bytes 786440 | tf_op jit(solution)/shard_map/ppermute | solution.py:651
  165.6 11.2 %collective-permute-start.37 = (bf16[256,512]{1,0:T(8,128)(2,1)S(1)}, bf16[256,512]{1,0:T(8,128)(2,1)S(1)}, u32[]{:S(2)}, u32[]{:S(2)}) collective-permute-start(bf16[256,512]{1,0:T(8,128)(2,1)S(1)} %get-tuple-element.285), channel_id=1, source_target_pairs={{0,1},{1,0},{2,4},{3,5},{4,2},{5,3},{6,7},{7,6},{8,9},{9,8},{10,12... | collective-permute-start | bytes 786440 | tf_op jit(solution)/shard_map/ppermute | solution.py:651
  166.0 16.5 %collective-permute-start.47 = (bf16[256,512]{1,0:T(8,128)(2,1)S(1)}, bf16[256,512]{1,0:T(8,128)(2,1)S(1)}, u32[]{:S(2)}, u32[]{:S(2)}) collective-permute-start(bf16[256,512]{1,0:T(8,128)(2,1)S(1)} %get-tuple-element.294), channel_id=1, source_target_pairs={{0,2},{1,3},{2,0},{3,1},{4,6},{5,7},{6,4},{7,5},{8,10},{9,11},{10,... | collective-permute-start | bytes 786440 | tf_op jit(solution)/shard_map/ppermute | solution.py:651
  171.6 16.5 %collective-permute-start.43 = (bf16[256,512]{1,0:T(8,128)(2,1)S(1)}, bf16[256,512]{1,0:T(8,128)(2,1)S(1)}, u32[]{:S(2)}, u32[]{:S(2)}) collective-permute-start(bf16[256,512]{1,0:T(8,128)(2,1)S(1)} %get-tuple-element.290), channel_id=1, source_target_pairs={{0,2},{1,3},{2,0},{3,1},{4,6},{5,7},{6,4},{7,5},{8,10},{9,11},{10,... | collective-permute-start | bytes 786440 | tf_op jit(solution)/shard_map/ppermute | solution.py:651
  176.9 14.4 %collective-permute-start.44 = (bf16[256,512]{1,0:T(8,128)(2,1)S(1)}, bf16[256,512]{1,0:T(8,128)(2,1)S(1)}, u32[]{:S(2)}, u32[]{:S(2)}) collective-permute-start(bf16[256,512]{1,0:T(8,128)(2,1)S(1)} %get-tuple-element.291), channel_id=1, source_target_pairs={{0,1},{1,0},{2,4},{3,5},{4,2},{5,3},{6,7},{7,6},{8,9},{9,8},{10,12... | collective-permute-start | bytes 786440 | tf_op jit(solution)/shard_map/ppermute | solution.py:651
  177.2 16.5 %collective-permute-start.38 = (bf16[256,512]{1,0:T(8,128)(2,1)S(1)}, bf16[256,512]{1,0:T(8,128)(2,1)S(1)}, u32[]{:S(2)}, u32[]{:S(2)}) collective-permute-start(bf16[256,512]{1,0:T(8,128)(2,1)S(1)} %get-tuple-element.286), channel_id=1, source_target_pairs={{0,2},{1,3},{2,0},{3,1},{4,6},{5,7},{6,4},{7,5},{8,10},{9,11},{10,... | collective-permute-start | bytes 786440 | tf_op jit(solution)/shard_map/ppermute | solution.py:651
  182.9 15.9 %collective-permute-start.49 = (bf16[256,512]{1,0:T(8,128)(2,1)S(1)}, bf16[256,512]{1,0:T(8,128)(2,1)S(1)}, u32[]{:S(2)}, u32[]{:S(2)}) collective-permute-start(bf16[256,512]{1,0:T(8,128)(2,1)S(1)} %get-tuple-element.296), channel_id=1, source_target_pairs={{0,2},{1,3},{2,0},{3,1},{4,6},{5,7},{6,4},{7,5},{8,10},{9,11},{10,... | collective-permute-start | bytes 786440 | tf_op jit(solution)/shard_map/ppermute | solution.py:651
  (29 other events, 218.4 us)

commit v3 on v2

--- a/solution.py
+++ b/solution.py
@@ -86,8 +86,8 @@
         refs = refs[3:]
     outs = [refs.pop(0) for _ in routes]
     if runs_f:
-        gate_f, up_f, x_f = refs[:3]
-        refs = refs[3:]
+        gate_f, up_f, x_f, hidden = refs[:4]
+        refs = refs[4:]
     if runs_b:
         new_grad, norms, terms = refs[:3]
         refs = refs[3:]
@@ -99,7 +99,7 @@
             copy = pltpu.make_async_copy(sources[number], targets[number], sems.at[number])
             copy.start()
             loads.append(copy)
-    x_b, gate_b, up_b, grad_in, normed, hidden, wide = refs
+    x_b, gate_b, up_b, grad_in, normed, wide = refs
     last = sections - 1
     units = w_gate.shape[1]
     index_f = tick - pick_of(place, starts_f)
@@ -260,7 +260,7 @@
         operands += kept
     out_shape = [shape_of(rows, width)] * len(routes)
     if runs_f:
-        out_shape += [shape_of(rows, units, dtype=f32)] * 2 + [shape_of(rows, width)]
+        out_shape += [shape_of(rows, units, dtype=f32)] * 2 + [shape_of(rows, width), shape_of(rows, units)]
     if runs_b:
         out_shape += [shape_of(rows, width), shape_of(rows, width), shape_of(rows, 3 * units)]
     loading = tick == 0
@@ -289,7 +289,6 @@
             pltpu.VMEM((rows, units), f32),
             pltpu.VMEM((rows, width), bf16),
             pltpu.VMEM((rows, width), bf16),
-            pltpu.VMEM((rows, units), bf16),
             pltpu.VMEM((rows, width), f32),
         ]
         + [pltpu.SemaphoreType.DMA((4,))] * loading,
@@ -307,7 +306,7 @@
     loaded = None
     if loading:
         rest, loaded = rest[:-3], rest[-3:]
-    kept = rest[:3] if runs_f else None
+    kept = rest[:4] if runs_f else None
     terms = rest[-3:] if runs_b else None
     return outs, kept, terms, loaded
 
@@ -352,9 +351,10 @@
     )(grad_in, x, terms, w_gate, w_up, after)
 
 
-def collect_call(micro, rows, sections, total, whole, sources):
+def collect_call(micro, rows, sections, total, whole, sources, forward=False):
     last = sections - 1
-    starts_b = starts_of(sections)[1]
+    first = starts_of(sections)[0 if forward else 1]
+    base = min(first)
     starts = [min(i * rows, total - rows) for i in range(micro)]
     whole = [] if whole is None else [whole]
     found = []
@@ -380,7 +380,7 @@
                     target[...] = refs[0][...]
                 else:
                     for i, start in enumerate(starts):
-                        target[start : start + rows, :] = pool[at_of[i + starts_b[at] - starts_b[last], at]][...]
+                        target[start : start + rows, :] = pool[at_of[i + first[at] - base, at]][...]
 
     operands = whole + found
     width = operands[-1].shape[1]
@@ -581,7 +581,7 @@
         for at in range(last):
             index = tick - starts_b[at]
             if 0 <= index < micro:
-                saved.append((at, kept[index + starts_f[at]]))
+                saved.append((at, kept[index + starts_f[at]][:3]))
         outs, kept[tick], terms, loaded = tick_call(
             tick,
             micro,
@@ -606,6 +606,8 @@
     all_in = collect_call(micro, rows, sections, total, arrays[1], arrivals)
     grads, norms, terms = [list(column) for column in zip(*history)]
     last_terms = terms[-1]
+    hiddens = [kept[n][3] for n in range(micro + starts_f[last])]
+    hiddens = collect_call(micro, rows, sections, total, None, hiddens, True)
     normed, terms = laid(None, norms), laid(None, terms)
     near = [(z, z ^ 1) for z in range(chips)]
     far = [(z, ((z + 1) ^ 1) - 1) for z in range(chips)]
@@ -624,11 +626,11 @@
             arrived.append(line(outs[1], far, chips))
         return outs[0], arrived
 
-    keep, send = weight_call(chips, all_in, terms, 0, units, [], True)
+    keep, send = weight_call(chips, all_in, hiddens, 0, units, [], True)
     quick = (keep, permute(send, {}, sections, lanes))
-    begin(1, [send])
     moving = {}
     out, moving[0] = advance(1, 0, [], quick)
+    begin(1, [out])
     begin(2, [out])
     out, moving[1] = advance(1, 1, [])
     begin(0, [out])

time: 200 us -> 200 us (level)
  transfers between devices with their start and end apart: 51 -> 51, of which waited for: 23 -> 22; matrix products, arithmetic and copies ran while one was open for 0% -> 0% of each run, Pallas kernels for 28% -> 28%
where the time goes in v3:
time: 200 us
  starting transfers between devices  85.7 us (43%)
  Pallas kernels  66.6 us (33%)
  waiting for transfers between devices  45.3 us (23%)
    ppermute x36, starting transfers between devices, permute(): return lax.ppermute(value, ('section', 'dp'), pairs)  61.6 us
    pallas_call x22, Pallas kernels, tick_call(): pl.pallas_call(functools.partial(tick_kernel, tick, micro, rows, sections...  47.3 us
    ppermute x15, starting transfers between devices, line(): return lax.ppermute(value, 'dp', route)  24.1 us
    ppermute x15, waiting for transfers between devices, line(): return lax.ppermute(value, 'dp', route)  23.4 us
    ppermute x36, waiting for transfers between devices, permute(): return lax.ppermute(value, ('section', 'dp'), pairs)  22 us
    pallas_call x4, Pallas kernels, weight_call(): pl.pallas_call(weight_kernel, out_shape=[shape_of(count, half, units)] *...  8.2 us
    pallas_call x9, Pallas kernels, step_call(): pl.pallas_call(functools.partial(step_kernel, step, chips), out_shape=[sh...  4.48 us
  transfers between devices with their start and end apart: 51, of which 22 were waited for; matrix products, arithmetic and copies ran while one was open for 0% of the time, Pallas kernels for 28%

profile of v3, /device:TPU:0, one launch (start us, length us, event | category | flops | bytes accessed | tf_op | source)
XLA Modules:
  0.0 200.1 jit_solution(12519350601497373027)
XLA Ops:
  2.2 4.3 %tick.22 = (bf16[48,2048]{1,0:T(8,128)(2,1)S(1)}, f32[48,512]{1,0:T(8,128)S(1)}, f32[48,512]{1,0:T(8,128)S(1)}, bf16[48,2048]{1,0:T(8,128)(2,1)S(1)}, bf16[48,51...) custom-call(bf16[480,2048]{1,0:T(8,128)(2,1)S(1)} %copy-done.1, ...), custom_call_target="tpu_custom_call" | custom-call | flops 301989888 | bytes 6291456 | tf_op jit(solution)/shard_map/tick/pallas_call | solution.py:281
  10.4 3.9 %collective-permute-done.refs_4_ = bf16[48,2048]{1,0:T(8,128)(2,1)S(1)} collective-permute-done((bf16[48,2048]{1,0:T(8,128)(2,1)S(1)}, bf16[48,2048]{1,0:T(8,128)(2,1)S(1)}, u32[]{:S(2)}, u32[]{:S(2)}) %collective-permute-start) | collective-permute-done | bytes 196640 | tf_op jit(solution)/shard_map/ppermute | solution.py:441
  47.4 4.4 %collective-permute-start.13 = (bf16[48,2048]{1,0:T(8,128)(2,1)S(1)}, bf16[48,2048]{1,0:T(8,128)(2,1)S(1)}, u32[]{:S(2)}, u32[]{:S(2)}) collective-permute-start(bf16[48,2048]{1,0:T(8,128)(2,1)S(1)} %get-tuple-element.200), channel_id=1, source_target_pairs={{0,8},{1,9},{2,10},{3,11},{4,12},{5,13},{6,14},{7,15},{8,0},{9,1},... | collective-permute-start | bytes 589832 | tf_op jit(solution)/shard_map/ppermute | solution.py:441
  52.9 6.6 %collective-permute-done.13.refs_4_ = bf16[48,2048]{1,0:T(8,128)(2,1)S(1)} collective-permute-done((bf16[48,2048]{1,0:T(8,128)(2,1)S(1)}, bf16[48,2048]{1,0:T(8,128)(2,1)S(1)}, u32[]{:S(2)}, u32[]{:S(2)}) %collective-permute-start.13) | collective-permute-done | bytes 196640 | tf_op jit(solution)/shard_map/ppermute | solution.py:441
  59.5 4.3 %collective-permute-start.18 = (bf16[48,2048]{1,0:T(8,128)(2,1)S(1)}, bf16[48,2048]{1,0:T(8,128)(2,1)S(1)}, u32[]{:S(2)}, u32[]{:S(2)}) collective-permute-start(bf16[48,2048]{1,0:T(8,128)(2,1)S(1)} %get-tuple-element.212), channel_id=1, source_target_pairs={{0,8},{1,9},{2,10},{3,11},{4,12},{5,13},{6,14},{7,15},{8,0},{9,1},... | collective-permute-start | bytes 589832 | tf_op jit(solution)/shard_map/ppermute | solution.py:441
  64.3 7.8 %collective-permute-start.21 = (bf16[48,2048]{1,0:T(8,128)(2,1)S(1)}, bf16[48,2048]{1,0:T(8,128)(2,1)S(1)}, u32[]{:S(2)}, u32[]{:S(2)}) collective-permute-start(bf16[48,2048]{1,0:T(8,128)(2,1)S(1)} %get-tuple-element.222), channel_id=1, source_target_pairs={{0,8},{1,9},{2,10},{3,11},{4,12},{5,13},{6,14},{7,15},{8,0},{9,1},... | collective-permute-start | bytes 589832 | tf_op jit(solution)/shard_map/ppermute | solution.py:441
  75.1 5.5 %collective-permute-start.23 = (bf16[48,2048]{1,0:T(8,128)(2,1)S(1)}, bf16[48,2048]{1,0:T(8,128)(2,1)S(1)}, u32[]{:S(2)}, u32[]{:S(2)}) collective-permute-start(bf16[48,2048]{1,0:T(8,128)(2,1)S(1)} %get-tuple-element.231), channel_id=1, source_target_pairs={{0,16},{1,17},{2,18},{3,19},{4,20},{5,21},{6,22},{7,23},{8,0},{9,1... | collective-permute-start | bytes 589832 | tf_op jit(solution)/shard_map/ppermute | solution.py:441
  84.5 4.5 %collective-permute-start.25 = (bf16[48,2048]{1,0:T(8,128)(2,1)S(1)}, bf16[48,2048]{1,0:T(8,128)(2,1)S(1)}, u32[]{:S(2)}, u32[]{:S(2)}) collective-permute-start(bf16[48,2048]{1,0:T(8,128)(2,1)S(1)} %get-tuple-element.237), channel_id=1, source_target_pairs={{0,16},{1,17},{2,18},{3,19},{4,20},{5,21},{6,22},{7,23},{8,0},{9,1... | collective-permute-start | bytes 589832 | tf_op jit(solution)/shard_map/ppermute | solution.py:441
  89.0 3.2 %tick.36 = (bf16[48,2048]{1,0:T(8,128)(2,1)S(1)}, f32[48,512]{1,0:T(8,128)}, f32[48,512]{1,0:T(8,128)}, bf16[48,2048]{1,0:T(8,128)(2,1)}, bf16[48,512]{1,0:T(8,1...) custom-call(bf16[480,2048]{1,0:T(8,128)(2,1)S(1)} %copy-done, ...), custom_call_target="tpu_custom_call" | custom-call | flops 603979776 | bytes 6291456 | tf_op jit(solution)/shard_map/tick/pallas_call | solution.py:281
  93.3 3.2 %tick.37 = (bf16[48,2048]{1,0:T(8,128)(2,1)S(1)}, f32[48,512]{1,0:T(8,128)}, f32[48,512]{1,0:T(8,128)}, bf16[48,2048]{1,0:T(8,128)(2,1)}, bf16[48,512]{1,0:T(8,1...) custom-call(bf16[480,2048]{1,0:T(8,128)(2,1)S(1)} %copy-done, ...), custom_call_target="tpu_custom_call" | custom-call | flops 603979776 | bytes 6291456 | tf_op jit(solution)/shard_map/tick/pallas_call | solution.py:281
  96.5 5.2 %collective-permute-start.27 = (bf16[48,2048]{1,0:T(8,128)(2,1)S(1)}, bf16[48,2048]{1,0:T(8,128)(2,1)S(1)}, u32[]{:S(2)}, u32[]{:S(2)}) collective-permute-start(bf16[48,2048]{1,0:T(8,128)(2,1)S(1)} %get-tuple-element.247), channel_id=1, source_target_pairs={{0,24},{1,25},{2,26},{3,27},{4,28},{5,29},{6,30},{7,31},{8,0},{9,1... | collective-permute-start | bytes 589832 | tf_op jit(solution)/shard_map/ppermute | solution.py:441
  104.2 4.6 %collective-permute-start.28 = (bf16[48,2048]{1,0:T(8,128)(2,1)S(1)}, bf16[48,2048]{1,0:T(8,128)(2,1)S(1)}, u32[]{:S(2)}, u32[]{:S(2)}) collective-permute-start(bf16[48,2048]{1,0:T(8,128)(2,1)S(1)} %get-tuple-element.252), channel_id=1, source_target_pairs={{0,16},{1,17},{2,18},{3,19},{4,20},{5,21},{6,22},{7,23},{8,0},{9,1... | collective-permute-start | bytes 589832 | tf_op jit(solution)/shard_map/ppermute | solution.py:441
  116.1 2.7 %collective-permute-start.30 = (bf16[48,2048]{1,0:T(8,128)(2,1)S(1)}, bf16[48,2048]{1,0:T(8,128)(2,1)S(1)}, u32[]{:S(2)}, u32[]{:S(2)}) collective-permute-start(bf16[48,2048]{1,0:T(8,128)(2,1)S(1)} %get-tuple-element.256), channel_id=1, source_target_pairs={{0,8},{1,9},{2,10},{3,11},{4,12},{5,13},{6,14},{7,15},{8,0},{9,1},... | collective-permute-start | bytes 589832 | tf_op jit(solution)/shard_map/ppermute | solution.py:441
  121.4 3.0 %collective-permute-start.31 = (bf16[48,2048]{1,0:T(8,128)(2,1)S(1)}, bf16[48,2048]{1,0:T(8,128)(2,1)S(1)}, u32[]{:S(2)}, u32[]{:S(2)}) collective-permute-start(bf16[48,2048]{1,0:T(8,128)(2,1)S(1)} %get-tuple-element.258), channel_id=1, source_target_pairs={{0,8},{1,9},{2,10},{3,11},{4,12},{5,13},{6,14},{7,15},{8,0},{9,1},... | collective-permute-start | bytes 589832 | tf_op jit(solution)/shard_map/ppermute | solution.py:441
  124.5 3.6 %collective-permute-done.31.refs_3_.refs_22_.grad_in = bf16[48,2048]{1,0:T(8,128)(2,1)S(1)} collective-permute-done((bf16[48,2048]{1,0:T(8,128)(2,1)S(1)}, bf16[48,2048]{1,0:T(8,128)(2,1)S(1)}, u32[]{:S(2)}, u32[]{:S(2)}) %collective-permute-start.31) | collective-permute-done | bytes 196640 | tf_op jit(solution)/shard_map/ppermute | solution.py:441
  144.4 3.2 %collective-permute-start.35 = (bf16[256,512]{1,0:T(8,128)(2,1)S(1)}, bf16[256,512]{1,0:T(8,128)(2,1)S(1)}, u32[]{:S(2)}, u32[]{:S(2)}) collective-permute-start(bf16[256,512]{1,0:T(8,128)(2,1)S(1)} %get-tuple-element.315), channel_id=1, source_target_pairs={{0,2},{1,3},{2,0},{3,1},{4,6},{5,7},{6,4},{7,5},{8,10},{9,11},{10,... | collective-permute-start | bytes 786440 | tf_op jit(solution)/shard_map/ppermute | solution.py:653
  149.7 5.1 %collective-permute-done.35.refs_0_ = bf16[256,512]{1,0:T(8,128)(2,1)S(1)} collective-permute-done((bf16[256,512]{1,0:T(8,128)(2,1)S(1)}, bf16[256,512]{1,0:T(8,128)(2,1)S(1)}, u32[]{:S(2)}, u32[]{:S(2)}) %collective-permute-start.35) | collective-permute-done | bytes 262176 | tf_op jit(solution)/shard_map/ppermute | solution.py:653
  157.2 3.2 %collective-permute-done.40.refs_0_ = bf16[256,512]{1,0:T(8,128)(2,1)S(1)} collective-permute-done((bf16[256,512]{1,0:T(8,128)(2,1)S(1)}, bf16[256,512]{1,0:T(8,128)(2,1)S(1)}, u32[]{:S(2)}, u32[]{:S(2)}) %collective-permute-start.40) | collective-permute-done | bytes 262176 | tf_op jit(solution)/shard_map/ppermute | solution.py:653
  162.8 3.2 %collective-permute-done.46.refs_0_ = bf16[256,512]{1,0:T(8,128)(2,1)S(1)} collective-permute-done((bf16[256,512]{1,0:T(8,128)(2,1)S(1)}, bf16[256,512]{1,0:T(8,128)(2,1)S(1)}, u32[]{:S(2)}, u32[]{:S(2)}) %collective-permute-start.46) | collective-permute-done | bytes 262176 | tf_op jit(solution)/shard_map/ppermute | solution.py:653
  166.3 3.7 %collective-permute-start.47 = (bf16[256,512]{1,0:T(8,128)(2,1)S(1)}, bf16[256,512]{1,0:T(8,128)(2,1)S(1)}, u32[]{:S(2)}, u32[]{:S(2)}) collective-permute-start(bf16[256,512]{1,0:T(8,128)(2,1)S(1)} %get-tuple-element.326), channel_id=1, source_target_pairs={{0,2},{1,3},{2,0},{3,1},{4,6},{5,7},{6,4},{7,5},{8,10},{9,11},{10,... | collective-permute-start | bytes 786440 | tf_op jit(solution)/shard_map/ppermute | solution.py:653
  172.0 3.7 %collective-permute-start.38 = (bf16[256,512]{1,0:T(8,128)(2,1)S(1)}, bf16[256,512]{1,0:T(8,128)(2,1)S(1)}, u32[]{:S(2)}, u32[]{:S(2)}) collective-permute-start(bf16[256,512]{1,0:T(8,128)(2,1)S(1)} %get-tuple-element.318), channel_id=1, source_target_pairs={{0,2},{1,3},{2,0},{3,1},{4,6},{5,7},{6,4},{7,5},{8,10},{9,11},{10,... | collective-permute-start | bytes 786440 | tf_op jit(solution)/shard_map/ppermute | solution.py:653
  177.6 3.7 %collective-permute-start.43 = (bf16[256,512]{1,0:T(8,128)(2,1)S(1)}, bf16[256,512]{1,0:T(8,128)(2,1)S(1)}, u32[]{:S(2)}, u32[]{:S(2)}) collective-permute-start(bf16[256,512]{1,0:T(8,128)(2,1)S(1)} %get-tuple-element.322), channel_id=1, source_target_pairs={{0,2},{1,3},{2,0},{3,1},{4,6},{5,7},{6,4},{7,5},{8,10},{9,11},{10,... | collective-permute-start | bytes 786440 | tf_op jit(solution)/shard_map/ppermute | solution.py:653
  183.2 3.7 %collective-permute-start.49 = (bf16[256,512]{1,0:T(8,128)(2,1)S(1)}, bf16[256,512]{1,0:T(8,128)(2,1)S(1)}, u32[]{:S(2)}, u32[]{:S(2)}) collective-permute-start(bf16[256,512]{1,0:T(8,128)(2,1)S(1)} %get-tuple-element.328), channel_id=1, source_target_pairs={{0,2},{1,3},{2,0},{3,1},{4,6},{5,7},{6,4},{7,5},{8,10},{9,11},{10,... | collective-permute-start | bytes 786440 | tf_op jit(solution)/shard_map/ppermute | solution.py:653
  195.1 4.0 %collective-permute-done.49.refs_0_ = bf16[256,512]{1,0:T(8,128)(2,1)S(1)} collective-permute-done((bf16[256,512]{1,0:T(8,128)(2,1)S(1)}, bf16[256,512]{1,0:T(8,128)(2,1)S(1)}, u32[]{:S(2)}, u32[]{:S(2)}) %collective-permute-start.49) | collective-permute-done | bytes 262176 | tf_op jit(solution)/shard_map/ppermute | solution.py:653
  (126 shorter events, 98.8 us)
Async XLA Ops:
  47.4 12.1 %collective-permute-start.13 = (bf16[48,2048]{1,0:T(8,128)(2,1)S(1)}, bf16[48,2048]{1,0:T(8,128)(2,1)S(1)}, u32[]{:S(2)}, u32[]{:S(2)}) collective-permute-start(bf16[48,2048]{1,0:T(8,128)(2,1)S(1)} %get-tuple-element.200), channel_id=1, source_target_pairs={{0,8},{1,9},{2,10},{3,11},{4,12},{5,13},{6,14},{7,15},{8,0},{9,1},... | collective-permute-start | bytes 589832 | tf_op jit(solution)/shard_map/ppermute | solution.py:441
  51.8 12.0 %collective-permute-start.14 = (bf16[48,2048]{1,0:T(8,128)(2,1)S(1)}, bf16[48,2048]{1,0:T(8,128)(2,1)S(1)}, u32[]{:S(2)}, u32[]{:S(2)}) collective-permute-start(bf16[48,2048]{1,0:T(8,128)(2,1)S(1)} %get-tuple-element.201), channel_id=1, source_target_pairs={{0,1},{1,0},{2,3},{3,2},{4,5},{5,4},{6,7},{7,6},{8,16},{9,17},{10,... | collective-permute-start | bytes 589832 | tf_op jit(solution)/shard_map/ppermute | solution.py:441
  51.8 11.9 %collective-permute-start.15 = (bf16[48,2048]{1,0:T(8,128)(2,1)S(1)}, bf16[48,2048]{1,0:T(8,128)(2,1)S(1)}, u32[]{:S(2)}, u32[]{:S(2)}) collective-permute-start(bf16[48,2048]{1,0:T(8,128)(2,1)S(1)} %get-tuple-element.202), channel_id=1, source_target_pairs={{0,1},{1,0},{2,3},{3,2},{4,5},{5,4},{6,7},{7,6},{8,9},{9,8},{10,11... | collective-permute-start | bytes 589832 | tf_op jit(solution)/shard_map/ppermute | solution.py:441
  52.3 12.0 %collective-permute-start.16 = (bf16[48,2048]{1,0:T(8,128)(2,1)S(1)}, bf16[48,2048]{1,0:T(8,128)(2,1)S(1)}, u32[]{:S(2)}, u32[]{:S(2)}) collective-permute-start(bf16[48,2048]{1,0:T(8,128)(2,1)S(1)} %get-tuple-element.210), channel_id=1, source_target_pairs={{0,1},{1,0},{2,3},{3,2},{4,5},{5,4},{6,7},{7,6},{8,16},{9,17},{10,... | collective-permute-start | bytes 589832 | tf_op jit(solution)/shard_map/ppermute | solution.py:441
  52.6 19.5 %collective-permute-start.17 = (bf16[48,2048]{1,0:T(8,128)(2,1)S(1)}, bf16[48,2048]{1,0:T(8,128)(2,1)S(1)}, u32[]{:S(2)}, u32[]{:S(2)}) collective-permute-start(bf16[48,2048]{1,0:T(8,128)(2,1)S(1)} %get-tuple-element.211), channel_id=1, source_target_pairs={{0,1},{1,0},{2,3},{3,2},{4,5},{5,4},{6,7},{7,6},{8,9},{9,8},{10,11... | collective-permute-start | bytes 589832 | tf_op jit(solution)/shard_map/ppermute | solution.py:441
  59.5 13.0 %collective-permute-start.18 = (bf16[48,2048]{1,0:T(8,128)(2,1)S(1)}, bf16[48,2048]{1,0:T(8,128)(2,1)S(1)}, u32[]{:S(2)}, u32[]{:S(2)}) collective-permute-start(bf16[48,2048]{1,0:T(8,128)(2,1)S(1)} %get-tuple-element.212), channel_id=1, source_target_pairs={{0,8},{1,9},{2,10},{3,11},{4,12},{5,13},{6,14},{7,15},{8,0},{9,1},... | collective-permute-start | bytes 589832 | tf_op jit(solution)/shard_map/ppermute | solution.py:441
  63.8 16.8 %collective-permute-start.19 = (bf16[48,2048]{1,0:T(8,128)(2,1)S(1)}, bf16[48,2048]{1,0:T(8,128)(2,1)S(1)}, u32[]{:S(2)}, u32[]{:S(2)}) collective-permute-start(bf16[48,2048]{1,0:T(8,128)(2,1)S(1)} %get-tuple-element.220), channel_id=1, source_target_pairs={{0,1},{1,0},{2,3},{3,2},{4,5},{5,4},{6,7},{7,6},{8,16},{9,17},{10,... | collective-permute-start | bytes 589832 | tf_op jit(solution)/shard_map/ppermute | solution.py:441
  64.0 16.6 %collective-permute-start.20 = (bf16[48,2048]{1,0:T(8,128)(2,1)S(1)}, bf16[48,2048]{1,0:T(8,128)(2,1)S(1)}, u32[]{:S(2)}, u32[]{:S(2)}) collective-permute-start(bf16[48,2048]{1,0:T(8,128)(2,1)S(1)} %get-tuple-element.221), channel_id=1, source_target_pairs={{0,1},{1,0},{2,3},{3,2},{4,5},{5,4},{6,7},{7,6},{8,9},{9,8},{10,11... | collective-permute-start | bytes 589832 | tf_op jit(solution)/shard_map/ppermute | solution.py:441
  64.3 17.7 %collective-permute-start.21 = (bf16[48,2048]{1,0:T(8,128)(2,1)S(1)}, bf16[48,2048]{1,0:T(8,128)(2,1)S(1)}, u32[]{:S(2)}, u32[]{:S(2)}) collective-permute-start(bf16[48,2048]{1,0:T(8,128)(2,1)S(1)} %get-tuple-element.222), channel_id=1, source_target_pairs={{0,8},{1,9},{2,10},{3,11},{4,12},{5,13},{6,14},{7,15},{8,0},{9,1},... | collective-permute-start | bytes 589832 | tf_op jit(solution)/shard_map/ppermute | solution.py:441
  75.0 14.0 %collective-permute-start.22 = (bf16[48,2048]{1,0:T(8,128)(2,1)S(1)}, bf16[48,2048]{1,0:T(8,128)(2,1)S(1)}, u32[]{:S(2)}, u32[]{:S(2)}) collective-permute-start(bf16[48,2048]{1,0:T(8,128)(2,1)S(1)} %get-tuple-element.230), channel_id=1, source_target_pairs={{0,1},{1,0},{2,3},{3,2},{4,5},{5,4},{6,7},{7,6},{8,9},{9,8},{10,11... | collective-permute-start | bytes 589832 | tf_op jit(solution)/shard_map/ppermute | solution.py:441
  75.1 14.0 %collective-permute-start.23 = (bf16[48,2048]{1,0:T(8,128)(2,1)S(1)}, bf16[48,2048]{1,0:T(8,128)(2,1)S(1)}, u32[]{:S(2)}, u32[]{:S(2)}) collective-permute-start(bf16[48,2048]{1,0:T(8,128)(2,1)S(1)} %get-tuple-element.231), channel_id=1, source_target_pairs={{0,16},{1,17},{2,18},{3,19},{4,20},{5,21},{6,22},{7,23},{8,0},{9,1... | collective-permute-start | bytes 589832 | tf_op jit(solution)/shard_map/ppermute | solution.py:441
  96.5 13.6 %collective-permute-start.27 = (bf16[48,2048]{1,0:T(8,128)(2,1)S(1)}, bf16[48,2048]{1,0:T(8,128)(2,1)S(1)}, u32[]{:S(2)}, u32[]{:S(2)}) collective-permute-start(bf16[48,2048]{1,0:T(8,128)(2,1)S(1)} %get-tuple-element.247), channel_id=1, source_target_pairs={{0,24},{1,25},{2,26},{3,27},{4,28},{5,29},{6,30},{7,31},{8,0},{9,1... | collective-permute-start | bytes 589832 | tf_op jit(solution)/shard_map/ppermute | solution.py:441
  143.1 23.0 %collective-permute-start.45 = (bf16[4,256,512]{2,1,0:T(8,128)(2,1)S(1)}, bf16[4,256,512]{2,1,0:T(8,128)(2,1)S(1)}, u32[]{:S(2)}, u32[]{:S(2)}) collective-permute-start(bf16[4,256,512]{2,1,0:T(8,128)(2,1)S(1)} %get-tuple-element.325), channel_id=1, source_target_pairs={{0,1},{1,0},{2,3},{3,2},{4,5},{5,4},{6,7},{7,6},{8,9},{9,8},{10,11... | collective-permute-start | bytes 3145736 | tf_op jit(solution)/shard_map/ppermute | solution.py:441
  147.6 12.8 %collective-permute-start.40 = (bf16[256,512]{1,0:T(8,128)(2,1)S(1)}, bf16[256,512]{1,0:T(8,128)(2,1)S(1)}, u32[]{:S(2)}, u32[]{:S(2)}) collective-permute-start(bf16[256,512]{1,0:T(8,128)(2,1)S(1)} %get-tuple-element.312.after.refs_0_), channel_id=1, source_target_pairs={{0,2},{1,3},{2,0},{3,1},{4,6},{5,7},{6,4},{7,5},{8,10},{9,11},{10,... | collective-permute-start | bytes 786440 | tf_op jit(solution)/shard_map/ppermute | solution.py:653
  147.7 18.4 %collective-permute-start.46 = (bf16[256,512]{1,0:T(8,128)(2,1)S(1)}, bf16[256,512]{1,0:T(8,128)(2,1)S(1)}, u32[]{:S(2)}, u32[]{:S(2)}) collective-permute-start(bf16[256,512]{1,0:T(8,128)(2,1)S(1)} %get-tuple-element.309.refs_0_), channel_id=1, source_target_pairs={{0,2},{1,3},{2,0},{3,1},{4,6},{5,7},{6,4},{7,5},{8,10},{9,11},{10,... | collective-permute-start | bytes 786440 | tf_op jit(solution)/shard_map/ppermute | solution.py:653
  155.1 16.6 %collective-permute-start.36 = (bf16[256,512]{1,0:T(8,128)(2,1)S(1)}, bf16[256,512]{1,0:T(8,128)(2,1)S(1)}, u32[]{:S(2)}, u32[]{:S(2)}) collective-permute-start(bf16[256,512]{1,0:T(8,128)(2,1)S(1)} %get-tuple-element.316), channel_id=1, source_target_pairs={{0,2},{1,3},{2,0},{3,1},{4,6},{5,7},{6,4},{7,5},{8,10},{9,11},{10,... | collective-permute-start | bytes 786440 | tf_op jit(solution)/shard_map/ppermute | solution.py:653
  157.2 14.5 %collective-permute-start.37 = (bf16[256,512]{1,0:T(8,128)(2,1)S(1)}, bf16[256,512]{1,0:T(8,128)(2,1)S(1)}, u32[]{:S(2)}, u32[]{:S(2)}) collective-permute-start(bf16[256,512]{1,0:T(8,128)(2,1)S(1)} %get-tuple-element.317), channel_id=1, source_target_pairs={{0,1},{1,0},{2,4},{3,5},{4,2},{5,3},{6,7},{7,6},{8,9},{9,8},{10,12... | collective-permute-start | bytes 786440 | tf_op jit(solution)/shard_map/ppermute | solution.py:653
  160.7 16.6 %collective-permute-start.41 = (bf16[256,512]{1,0:T(8,128)(2,1)S(1)}, bf16[256,512]{1,0:T(8,128)(2,1)S(1)}, u32[]{:S(2)}, u32[]{:S(2)}) collective-permute-start(bf16[256,512]{1,0:T(8,128)(2,1)S(1)} %get-tuple-element.320), channel_id=1, source_target_pairs={{0,2},{1,3},{2,0},{3,1},{4,6},{5,7},{6,4},{7,5},{8,10},{9,11},{10,... | collective-permute-start | bytes 786440 | tf_op jit(solution)/shard_map/ppermute | solution.py:653
  166.0 11.2 %collective-permute-start.42 = (bf16[256,512]{1,0:T(8,128)(2,1)S(1)}, bf16[256,512]{1,0:T(8,128)(2,1)S(1)}, u32[]{:S(2)}, u32[]{:S(2)}) collective-permute-start(bf16[256,512]{1,0:T(8,128)(2,1)S(1)} %get-tuple-element.321), channel_id=1, source_target_pairs={{0,1},{1,0},{2,4},{3,5},{4,2},{5,3},{6,7},{7,6},{8,9},{9,8},{10,12... | collective-permute-start | bytes 786440 | tf_op jit(solution)/shard_map/ppermute | solution.py:653
  166.3 16.5 %collective-permute-start.47 = (bf16[256,512]{1,0:T(8,128)(2,1)S(1)}, bf16[256,512]{1,0:T(8,128)(2,1)S(1)}, u32[]{:S(2)}, u32[]{:S(2)}) collective-permute-start(bf16[256,512]{1,0:T(8,128)(2,1)S(1)} %get-tuple-element.326), channel_id=1, source_target_pairs={{0,2},{1,3},{2,0},{3,1},{4,6},{5,7},{6,4},{7,5},{8,10},{9,11},{10,... | collective-permute-start | bytes 786440 | tf_op jit(solution)/shard_map/ppermute | solution.py:653
  172.0 16.5 %collective-permute-start.38 = (bf16[256,512]{1,0:T(8,128)(2,1)S(1)}, bf16[256,512]{1,0:T(8,128)(2,1)S(1)}, u32[]{:S(2)}, u32[]{:S(2)}) collective-permute-start(bf16[256,512]{1,0:T(8,128)(2,1)S(1)} %get-tuple-element.318), channel_id=1, source_target_pairs={{0,2},{1,3},{2,0},{3,1},{4,6},{5,7},{6,4},{7,5},{8,10},{9,11},{10,... | collective-permute-start | bytes 786440 | tf_op jit(solution)/shard_map/ppermute | solution.py:653
  177.3 14.4 %collective-permute-start.39 = (bf16[256,512]{1,0:T(8,128)(2,1)S(1)}, bf16[256,512]{1,0:T(8,128)(2,1)S(1)}, u32[]{:S(2)}, u32[]{:S(2)}) collective-permute-start(bf16[256,512]{1,0:T(8,128)(2,1)S(1)} %get-tuple-element.319), channel_id=1, source_target_pairs={{0,1},{1,0},{2,4},{3,5},{4,2},{5,3},{6,7},{7,6},{8,9},{9,8},{10,12... | collective-permute-start | bytes 786440 | tf_op jit(solution)/shard_map/ppermute | solution.py:653
  177.6 16.5 %collective-permute-start.43 = (bf16[256,512]{1,0:T(8,128)(2,1)S(1)}, bf16[256,512]{1,0:T(8,128)(2,1)S(1)}, u32[]{:S(2)}, u32[]{:S(2)}) collective-permute-start(bf16[256,512]{1,0:T(8,128)(2,1)S(1)} %get-tuple-element.322), channel_id=1, source_target_pairs={{0,2},{1,3},{2,0},{3,1},{4,6},{5,7},{6,4},{7,5},{8,10},{9,11},{10,... | collective-permute-start | bytes 786440 | tf_op jit(solution)/shard_map/ppermute | solution.py:653
  183.2 15.8 %collective-permute-start.49 = (bf16[256,512]{1,0:T(8,128)(2,1)S(1)}, bf16[256,512]{1,0:T(8,128)(2,1)S(1)}, u32[]{:S(2)}, u32[]{:S(2)}) collective-permute-start(bf16[256,512]{1,0:T(8,128)(2,1)S(1)} %get-tuple-element.328), channel_id=1, source_target_pairs={{0,2},{1,3},{2,0},{3,1},{4,6},{5,7},{6,4},{7,5},{8,10},{9,11},{10,... | collective-permute-start | bytes 786440 | tf_op jit(solution)/shard_map/ppermute | solution.py:653
  (29 other events, 212.2 us)
